TPU v7x, 32 devices: a whole 2x2x4 slice. The times are simulated.
32 devices in a mesh: fsdp: 4 (over y, x), ctx: 4 (over z), tp: 2 (over core).
Axes of the slice: x: 2, y: 2, z: 4, core: 2. Of those that a mesh axis runs over, the one named last changes fastest.
Arguments:
- image_input: bfloat16 [4, 2048, 768], P('fsdp', 'ctx'), may hold values from -6 to 6
- image_segments: int32 [4, 2048], P('fsdp'), may hold values from 0 to 5, never falling along the last dimension, each value on 1 to 1536 neighbouring positions
- image_cotangent: bfloat16 [4, 2048, 768], P('fsdp', 'ctx'), may hold values from -6 to 6
- image_gains: bfloat16 [2, 768], P(None, 'fsdp'), may hold values from 0.099609375 to 1.8984375
- image_shifts: bfloat16 [4, 768], P(None, 'fsdp'), may hold values from -3 to 3
- image_head_bias: bfloat16 [2, 2304], P('tp', 'fsdp'), may hold values from -3 to 3
- image_qkv_weight: bfloat16 [3, 768, 768], P(None, 'fsdp', 'tp'), may hold values from -0.21875 to 0.21875
- image_proj_weight: bfloat16 [768, 768], P('tp', 'fsdp'), may hold values from -0.875 to 0.875
- image_up_weight: bfloat16 [768, 3072], P('fsdp', 'tp'), may hold values from -0.21875 to 0.21875
- image_down_weight: bfloat16 [3072, 768], P('tp', 'fsdp'), may hold values from -0.109375 to 0.109375
- text_input: bfloat16 [4, 2048, 512], P('fsdp', 'ctx'), may hold values from -6 to 6
- text_segments: int32 [4, 2048], P('fsdp'), may hold values from 0 to 5, never falling along the last dimension, each value on 1 to 1536 neighbouring positions
- text_cotangent: bfloat16 [4, 2048, 512], P('fsdp', 'ctx'), may hold values from -6 to 6
- text_gains: bfloat16 [2, 512], P(None, 'fsdp'), may hold values from 0.099609375 to 1.8984375
- text_shifts: bfloat16 [4, 512], P(None, 'fsdp'), may hold values from -3 to 3
- text_head_bias: bfloat16 [2, 1536], P('tp', 'fsdp'), may hold values from -3 to 3
- text_qkv_weight: bfloat16 [3, 512, 512], P(None, 'fsdp', 'tp'), may hold values from -0.25 to 0.25
- text_proj_weight: bfloat16 [512, 512], P('tp', 'fsdp'), may hold values from -1 to 1
- text_up_weight: bfloat16 [512, 2048], P('fsdp', 'tp'), may hold values from -0.25 to 0.25
- text_down_weight: bfloat16 [2048, 512], P('tp', 'fsdp'), may hold values from -0.125 to 0.125
Outputs:
- image_output: bfloat16 [4, 2048, 768], P('fsdp', 'ctx')
- image_input_grad: float32 [4, 2048, 768], P('fsdp', 'ctx')
- image_gains_grad: float32 [2, 768], P(None, 'fsdp')
- image_shifts_grad: float32 [4, 768], P(None, 'fsdp')
- image_head_bias_grad: float32 [2, 2304], P('tp', 'fsdp')
- image_qkv_grad: float32 [3, 768, 768], P(None, 'fsdp', 'tp')
- image_proj_grad: float32 [768, 768], P('tp', 'fsdp')
- image_up_grad: float32 [768, 3072], P('fsdp', 'tp')
- image_down_grad: float32 [3072, 768], P('tp', 'fsdp')
- text_output: bfloat16 [4, 2048, 512], P('fsdp', 'ctx')
- text_input_grad: float32 [4, 2048, 512], P('fsdp', 'ctx')
- text_gains_grad: float32 [2, 512], P(None, 'fsdp')
- text_shifts_grad: float32 [4, 512], P(None, 'fsdp')
- text_head_bias_grad: float32 [2, 1536], P('tp', 'fsdp')
- text_qkv_grad: float32 [3, 512, 512], P(None, 'fsdp', 'tp')
- text_proj_grad: float32 [512, 512], P('tp', 'fsdp')
- text_up_grad: float32 [512, 2048], P('fsdp', 'tp')
- text_down_grad: float32 [2048, 512], P('tp', 'fsdp')
Inputs may be any that keep to these rules, and one draw needn't show every extreme that they name: `image_segments`: along each sequence segment numbers never fall; every document has 1 to 1536 tokens, and one has exactly that many. `text_segments`: along each sequence segment numbers never fall; every document has 1 to 1536 tokens, and one has exactly that many.
All inputs are finite; a program needn't handle non-finite values.
Results may differ from a plain program's by a relative error of at most 0.012.
Values may be sent and summed in bfloat16 or wider, within the bound.
A program may use at most 128 MiB of HBM per device.

v0:
```python
import jax
import jax.numpy as jnp
from jax import lax
from jax.sharding import PartitionSpec as P

HD = 64


def layer_stats(rows):
    row_mean = jnp.mean(rows, axis=-1, keepdims=True)
    centred = rows - row_mean
    inv_std = lax.rsqrt(jnp.mean(centred * centred, axis=-1, keepdims=True) + 1e-05)
    return (centred * inv_std, inv_std)


def norm_back(grad_normed_out, normed, inv_std, gain):
    scaled = grad_normed_out * gain
    return inv_std * (
        scaled
        - jnp.mean(scaled, axis=-1, keepdims=True)
        - normed * jnp.mean(scaled * normed, axis=-1, keepdims=True)
    )


def tensor_sum(partial_rows):
    return lax.psum(partial_rows, "tp")


def run_block(
    rows_in,
    seg_row,
    cotangent,
    gains,
    shifts,
    head_bias,
    qkv_weight,
    proj_weight,
    up_weight,
    down_weight,
    causal,
):
    gain_full, shift_full, bias_full, qkv_full, proj_full, up_full, down_full = (
        lax.all_gather(gains, "fsdp", axis=1, tiled=True),
        lax.all_gather(shifts, "fsdp", axis=1, tiled=True),
        lax.all_gather(head_bias, "fsdp", axis=1, tiled=True),
        lax.all_gather(qkv_weight, "fsdp", axis=1, tiled=True),
        lax.all_gather(proj_weight, "fsdp", axis=1, tiled=True),
        lax.all_gather(up_weight, "fsdp", axis=0, tiled=True),
        lax.all_gather(down_weight, "fsdp", axis=1, tiled=True),
    )
    gain_vals = gain_full.astype(jnp.float32)
    shift_vals = shift_full.astype(jnp.float32)
    bias_vals = bias_full[0].astype(jnp.float32)
    tp_width = qkv_full.shape[2]
    local_rows = rows_in.shape[1]
    seq_length = seg_row.shape[1]
    head_local = tp_width // HD
    rows = rows_in[0].astype(jnp.float32)
    row_start = lax.axis_index("ctx") * local_rows
    seg_all = seg_row[0]
    seg_query = lax.dynamic_slice_in_dim(seg_all, row_start, local_rows)
    query_pos = row_start + jnp.arange(local_rows, dtype=jnp.int32)
    key_pos = jnp.arange(seq_length, dtype=jnp.int32)
    allowed = seg_query[:, None] == seg_all[None, :]
    if causal:
        allowed = jnp.logical_and(allowed, key_pos[None, :] <= query_pos[:, None])

    def to_heads(matrix):
        return matrix.reshape(matrix.shape[0], head_local, HD).transpose(1, 0, 2)

    def from_heads(stacked):
        return stacked.transpose(1, 0, 2).reshape(stacked.shape[1], head_local * HD)

    normed_one, inv_one = layer_stats(rows)
    first_in = (normed_one * gain_vals[0] + shift_vals[0]).astype(jnp.bfloat16)
    queries = (
        jnp.dot(first_in, qkv_full[0], preferred_element_type=jnp.float32) + bias_vals[:tp_width]
    ).astype(jnp.bfloat16)
    key_rows = jnp.dot(first_in, qkv_full[1], preferred_element_type=jnp.float32).astype(
        jnp.bfloat16
    )
    values = (
        jnp.dot(first_in, qkv_full[2], preferred_element_type=jnp.float32)
        + bias_vals[tp_width : 2 * tp_width]
    ).astype(jnp.bfloat16)
    key_all, value_all = (
        lax.all_gather(key_rows, "ctx", axis=0, tiled=True),
        lax.all_gather(values, "ctx", axis=0, tiled=True),
    )
    query_heads = to_heads(queries)
    key_heads = to_heads(key_all)
    value_heads = to_heads(value_all)

    def attend(head_items):
        query_h, key_h, value_h = head_items
        scores = jnp.einsum("qd,kd->qk", query_h, key_h, preferred_element_type=jnp.float32) * 0.125
        scores = jnp.where(allowed, scores, -1e30)
        row_top = jnp.max(scores, axis=-1, keepdims=True)
        weights = jnp.exp(scores - row_top)
        row_total = jnp.sum(weights, axis=-1, keepdims=True)
        weights_low = (weights / row_total).astype(jnp.bfloat16)
        mixed_h = jnp.einsum("qk,kd->qd", weights_low, value_h, preferred_element_type=jnp.float32)
        return (mixed_h.astype(jnp.bfloat16), row_top[:, 0] + jnp.log(row_total[:, 0]))

    mixed_heads, log_totals = lax.map(attend, (query_heads, key_heads, value_heads))
    mixed = from_heads(mixed_heads)
    middle = (
        rows
        + tensor_sum(jnp.dot(mixed, proj_full, preferred_element_type=jnp.float32))
        + shift_vals[1]
    )
    normed_two, inv_two = layer_stats(middle)
    second_in = (normed_two * gain_vals[1] + shift_vals[2]).astype(jnp.bfloat16)
    hidden = (
        jnp.dot(second_in, up_full, preferred_element_type=jnp.float32) + bias_vals[2 * tp_width :]
    )
    sigma = jax.nn.sigmoid(1.702 * hidden)
    activated = (hidden * sigma).astype(jnp.bfloat16)
    output = (
        middle
        + tensor_sum(jnp.dot(activated, down_full, preferred_element_type=jnp.float32))
        + shift_vals[3]
    )
    grad_out = cotangent[0].astype(jnp.float32)
    grad_down_bias = jnp.sum(grad_out, axis=0)
    grad_branch = grad_out.astype(jnp.bfloat16)
    grad_down = jnp.einsum("tf,td->fd", activated, grad_branch, preferred_element_type=jnp.float32)
    grad_act = jnp.einsum("td,fd->tf", grad_branch, down_full, preferred_element_type=jnp.float32)
    grad_hidden = (grad_act * (sigma + 1.702 * hidden * sigma * (1.0 - sigma))).astype(jnp.bfloat16)
    grad_up_bias = jnp.sum(grad_hidden.astype(jnp.float32), axis=0)
    grad_up = jnp.einsum("td,tf->df", second_in, grad_hidden, preferred_element_type=jnp.float32)
    grad_second = tensor_sum(
        jnp.einsum("tf,df->td", grad_hidden, up_full, preferred_element_type=jnp.float32)
    )
    grad_gain_two = jnp.sum(grad_second * normed_two, axis=0)
    grad_shift_two = jnp.sum(grad_second, axis=0)
    grad_middle = grad_out + norm_back(grad_second, normed_two, inv_two, gain_vals[1])
    grad_proj_bias = jnp.sum(grad_middle, axis=0)
    grad_attn = grad_middle.astype(jnp.bfloat16)
    grad_proj = jnp.einsum("tc,td->cd", mixed, grad_attn, preferred_element_type=jnp.float32)
    grad_mixed = jnp.einsum(
        "td,cd->tc", grad_attn, proj_full, preferred_element_type=jnp.float32
    ).astype(jnp.bfloat16)

    def attend_back(head_items):
        query_h, key_h, value_h, grad_h, log_total = head_items
        scores = jnp.einsum("qd,kd->qk", query_h, key_h, preferred_element_type=jnp.float32) * 0.125
        weights = jnp.where(allowed, jnp.exp(scores - log_total[:, None]), 0.0)
        grad_weights = jnp.einsum("qd,kd->qk", grad_h, value_h, preferred_element_type=jnp.float32)
        row_delta = jnp.sum(weights * grad_weights, axis=-1, keepdims=True)
        grad_scores = (weights * (grad_weights - row_delta)).astype(jnp.bfloat16)
        grad_query_h = (
            jnp.einsum("qk,kd->qd", grad_scores, key_h, preferred_element_type=jnp.float32) * 0.125
        )
        grad_key_h = (
            jnp.einsum("qk,qd->kd", grad_scores, query_h, preferred_element_type=jnp.float32)
            * 0.125
        )
        grad_value_h = jnp.einsum(
            "qk,qd->kd", weights.astype(jnp.bfloat16), grad_h, preferred_element_type=jnp.float32
        )
        return (grad_query_h, grad_key_h, grad_value_h)

    query_parts, key_parts, value_parts = lax.map(
        attend_back, (query_heads, key_heads, value_heads, to_heads(grad_mixed), log_totals)
    )
    key_sum, value_sum = (
        lax.psum_scatter(from_heads(key_parts), "ctx", scatter_dimension=0, tiled=True),
        lax.psum_scatter(from_heads(value_parts), "ctx", scatter_dimension=0, tiled=True),
    )
    grad_query = from_heads(query_parts).astype(jnp.bfloat16)
    grad_key = key_sum.astype(jnp.bfloat16)
    grad_value = value_sum.astype(jnp.bfloat16)
    grad_qkv = jnp.stack(
        [
            jnp.einsum("td,tc->dc", first_in, grad_query, preferred_element_type=jnp.float32),
            jnp.einsum("td,tc->dc", first_in, grad_key, preferred_element_type=jnp.float32),
            jnp.einsum("td,tc->dc", first_in, grad_value, preferred_element_type=jnp.float32),
        ]
    )
    grad_head = jnp.concatenate(
        [
            jnp.sum(grad_query.astype(jnp.float32), axis=0),
            jnp.sum(grad_value.astype(jnp.float32), axis=0),
            grad_up_bias,
        ]
    )[None, :]
    grad_first_part = jnp.einsum(
        "tc,dc->td", grad_query, qkv_full[0], preferred_element_type=jnp.float32
    )
    grad_first_part = grad_first_part + jnp.einsum(
        "tc,dc->td", grad_key, qkv_full[1], preferred_element_type=jnp.float32
    )
    grad_first_part = grad_first_part + jnp.einsum(
        "tc,dc->td", grad_value, qkv_full[2], preferred_element_type=jnp.float32
    )
    grad_first = tensor_sum(grad_first_part)
    grad_gain_one = jnp.sum(grad_first * normed_one, axis=0)
    grad_shift_one = jnp.sum(grad_first, axis=0)
    grad_rows = grad_middle + norm_back(grad_first, normed_one, inv_one, gain_vals[0])
    grad_gains = jnp.stack([grad_gain_one, grad_gain_two])
    grad_shifts = jnp.stack([grad_shift_one, grad_proj_bias, grad_shift_two, grad_down_bias])
    share_gains, share_shifts, share_head, share_qkv, share_proj, share_up, share_down = (
        lax.psum_scatter(grad_gains, "fsdp", scatter_dimension=1, tiled=True),
        lax.psum_scatter(grad_shifts, "fsdp", scatter_dimension=1, tiled=True),
        lax.psum_scatter(grad_head, "fsdp", scatter_dimension=1, tiled=True),
        lax.psum_scatter(grad_qkv, "fsdp", scatter_dimension=1, tiled=True),
        lax.psum_scatter(grad_proj, "fsdp", scatter_dimension=1, tiled=True),
        lax.psum_scatter(grad_up, "fsdp", scatter_dimension=0, tiled=True),
        lax.psum_scatter(grad_down, "fsdp", scatter_dimension=1, tiled=True),
    )
    owned = lax.psum(
        (share_gains, share_shifts, share_head, share_qkv, share_proj, share_up, share_down), "ctx"
    )
    return (output.astype(jnp.bfloat16)[None], grad_rows[None]) + tuple(owned)


def on_device(
    image_input,
    image_segments,
    image_cotangent,
    image_gains,
    image_shifts,
    image_head_bias,
    image_qkv_weight,
    image_proj_weight,
    image_up_weight,
    image_down_weight,
    text_input,
    text_segments,
    text_cotangent,
    text_gains,
    text_shifts,
    text_head_bias,
    text_qkv_weight,
    text_proj_weight,
    text_up_weight,
    text_down_weight,
):
    image_results = run_block(
        image_input,
        image_segments,
        image_cotangent,
        image_gains,
        image_shifts,
        image_head_bias,
        image_qkv_weight,
        image_proj_weight,
        image_up_weight,
        image_down_weight,
        False,
    )
    text_results = run_block(
        text_input,
        text_segments,
        text_cotangent,
        text_gains,
        text_shifts,
        text_head_bias,
        text_qkv_weight,
        text_proj_weight,
        text_up_weight,
        text_down_weight,
        True,
    )
    return image_results + text_results


def solution(mesh):
    return jax.shard_map(
        on_device,
        mesh=mesh,
        in_specs=(
            P("fsdp", "ctx", None),
            P("fsdp", None),
            P("fsdp", "ctx", None),
            P(None, "fsdp"),
            P(None, "fsdp"),
            P("tp", "fsdp"),
            P(None, "fsdp", "tp"),
            P("tp", "fsdp"),
            P("fsdp", "tp"),
            P("tp", "fsdp"),
            P("fsdp", "ctx", None),
            P("fsdp", None),
            P("fsdp", "ctx", None),
            P(None, "fsdp"),
            P(None, "fsdp"),
            P("tp", "fsdp"),
            P(None, "fsdp", "tp"),
            P("tp", "fsdp"),
            P("fsdp", "tp"),
            P("tp", "fsdp"),
        ),
        out_specs=(
            P("fsdp", "ctx", None),
            P("fsdp", "ctx", None),
            P(None, "fsdp"),
            P(None, "fsdp"),
            P("tp", "fsdp"),
            P(None, "fsdp", "tp"),
            P("tp", "fsdp"),
            P("fsdp", "tp"),
            P("tp", "fsdp"),
            P("fsdp", "ctx", None),
            P("fsdp", "ctx", None),
            P(None, "fsdp"),
            P(None, "fsdp"),
            P("tp", "fsdp"),
            P(None, "fsdp", "tp"),
            P("tp", "fsdp"),
            P("fsdp", "tp"),
            P("tp", "fsdp"),
        ),
        check_vma=False,
    )
```

profile of v0, /device:TPU:0, one launch (start us, length us, event | category | flops | bytes accessed | tf_op | source)
XLA Modules:
  0.0 1437.3 jit_solution(6078367909397916896)
XLA Ops:
  8.0 9.5 all_gather.63
  17.5 7.9 all_gather.66
  25.4 7.2 all_gather.64
  33.9 16.2 %all_gather.65 = bf16[3,512,256]{2,1,0:T(8,128)(2,1)S(1)} all-gather(bf16[3,128,256]{2,1,0:T(8,128)(2,1)} %param.44), channel_id=1, replica_groups=mesh['fsdp'=4,'ctx'=4,'tp'=2] {'fsdp'}, dimensions={1}, use_global_device_ids=true | all-gather | bytes 983040 | tf_op jit(solution)/shard_map/all_gather | solution.py:46
  53.6 7.6 all-gather.1
  61.4 7.5 all-gather
  70.5 9.3 all-reduce
  85.0 8.5 all_gather.69
  93.5 9.8 all_gather.60
  116.4 30.7 %while.58 = (s32[]{:T(128)}, bf16[4,512,64]{1,2,0:T(8,128)(2,1)S(1)}, f32[4,512]{1,0:T(4,128)S(1)}, bf16[4,512,64]{2,1,0:T(8,128)(2,1)}, bf16[4,2048,64]{2,1,0:T...) while((s32[]{:T(128)}, ...), condition=%wide.region_49.50_spmd.clone, body=%wide.region_46.49_spmd.clone.sunk | while | flops 280002048 | bytes 30640268 | solution.py:105
  153.2 4.1 copy.88
  157.3 29.5 %all-gather.14.cloned.1.call-done = bf16[2048,384]{1,0:T(8,128)(2,1)} async-done(((bf16[512,384]{1,0:T(8,128)(2,1)}), bf16[2048,384]{1,0:T(8,128)(2,1)}) %all-gather.14.cloned.1.call-update) | async-done | bytes 1572880 | tf_op jit(solution)/shard_map/all_gather | solution.py:87
  189.4 4.2 copy.87
  193.5 43.0 %while.56 = (s32[]{:T(128)}, bf16[6,512,64]{1,2,0:T(8,128)(2,1)S(1)}, f32[6,512]{1,0:T(8,128)S(1)}, bf16[6,512,64]{2,1,0:T(8,128)(2,1)S(1)}, bf16[6,2048,64]{2,1...) while((s32[]{:T(128)}, ...), condition=%wide.region_5.6_spmd.clone, body=%wide.region_2.5_spmd.clone.sunk | while | flops 277904896 | bytes 30638212 | solution.py:105
  241.9 17.8 %all-reduce.17.cloned.1.call-done = (f32[512,768]{1,0:T(8,128)}, f32[512,512]{1,0:T(8,128)}) async-done(((f32[512,768]{1,0:T(8,128)}, f32[512,512]{1,0:T(8,128)}), (f32[512,768]{1,0:T(8,128)}, f32[512,512]{1,0:T(8,128)})) %all-reduce.17.cloned.1.call-update) | async-done | bytes 2621456 | tf_op jit(solution)/shard_map/psum | solution.py:26
  262.1 27.4 %all-gather.26.cloned.1.call-done = bf16[512,1024]{1,0:T(8,128)(2,1)} async-done(((bf16[128,1024]{1,0:T(8,128)(2,1)}), bf16[512,1024]{1,0:T(8,128)(2,1)}) %all-gather.26.cloned.1.call-update) | async-done | bytes 1048592 | tf_op jit(solution)/shard_map/all_gather | solution.py:48
  289.5 3.9 multiply_convert_fusion.4
  293.4 24.6 %all-gather.28.cloned.1.call-done = bf16[1024,512]{1,0:T(8,128)(2,1)} async-done(((bf16[1024,128]{1,0:T(8,128)(2,1)}), bf16[1024,512]{1,0:T(8,128)(2,1)}) %all-gather.28.cloned.1.call-update) | async-done | bytes 1048592 | tf_op jit(solution)/shard_map/all_gather | solution.py:49
  318.0 3.8 convert_reduce_fusion.2
  324.5 33.0 %all-gather.18.cloned.1.call-done = bf16[768,1536]{1,0:T(8,128)(2,1)} async-done(((bf16[192,1536]{1,0:T(8,128)(2,1)}), bf16[768,1536]{1,0:T(8,128)(2,1)}) %all-gather.18.cloned.1.call-update) | async-done | bytes 2359312 | tf_op jit(solution)/shard_map/all_gather | solution.py:48
  357.5 4.8 convolution_add_fusion
  362.3 34.5 %all-gather.20.cloned.1.call-done = bf16[1536,768]{0,1:T(8,128)(2,1)} async-done(((bf16[1536,192]{0,1:T(8,128)(2,1)}), bf16[1536,768]{0,1:T(8,128)(2,1)}) %all-gather.20.cloned.1.call-update) | async-done | bytes 2359312 | tf_op jit(solution)/shard_map/all_gather | solution.py:49
  396.8 5.6 convert_reduce_fusion
  406.5 22.1 %all-reduce.15.cloned.1.call-done = (f32[512,768]{1,0:T(8,128)}, f32[512,512]{1,0:T(8,128)}) async-done(((f32[512,768]{1,0:T(8,128)}, f32[512,512]{1,0:T(8,128)}), (f32[512,768]{1,0:T(8,128)}, f32[512,512]{1,0:T(8,128)})) %all-reduce.15.cloned.1.call-update) | async-done | bytes 2621456 | tf_op jit(solution)/shard_map/psum | solution.py:26
  435.4 31.2 %while.59 = (s32[]{:T(128)}, bf16[4,512,64]{1,2,0:T(8,128)(2,1)S(1)}, f32[4,2048,64]{1,2,0:T(8,128)}, f32[4,2048,64]{1,2,0:T(8,128)}, bf16[4,512,64]{2,1,0:T(8,1...) while((s32[]{:T(128)}, ...), condition=%wide.region_59.60_spmd.clone, body=%wide.region_57.59_spmd.clone.sunk | while | flops 683834880 | bytes 40004792 | solution.py:164
  474.9 65.2 %while.57 = (s32[]{:T(128)}, bf16[6,512,64]{1,2,0:T(8,128)(2,1)}, f32[6,2048,64]{1,2,0:T(8,128)}, f32[6,2048,64]{1,2,0:T(8,128)}, bf16[6,512,64]{2,1,0:T(8,128)(...) while((s32[]{:T(128)}, bf16[6,512,64]{1,2,0:T(8,128)(2,1)}, ...), condition=%wide.region_15.16_spmd.clone, body=%wide.region_13.15_spmd.clone.sunk | while | flops 681737728 | bytes 34759800 | solution.py:164
  544.3 4.9 fusion.171
  560.1 59.0 %reduce-scatter.31.cloned.1.call-done = f32[512,384]{0,1:T(8,128)} async-done(((f32[2048,384]{0,1:T(8,128)}), f32[512,384]{0,1:T(8,128)}) %reduce-scatter.31.cloned.1.call-update) | async-done | bytes 786448 | tf_op jit(solution)/shard_map/reduce_scatter | solution.py:168
  622.2 59.4 %reduce-scatter.33.cloned.1.call-done = f32[512,384]{0,1:T(8,128)} async-done(((f32[2048,384]{0,1:T(8,128)}), f32[512,384]{0,1:T(8,128)}) %reduce-scatter.33.cloned.1.call-update) | async-done | bytes 786448 | tf_op jit(solution)/shard_map/reduce_scatter | solution.py:169
  681.6 4.1 add_add_fusion
  700.4 5.1 fusion.170
  706.7 6.2 fusion.139
  739.9 5.8 reduce-scatter.49.cloned.1.call-done
  745.8 38.0 %reduce-scatter.51.cloned.1.call-done = f32[128,1024]{1,0:T(8,128)} async-done(((f32[512,1024]{1,0:T(8,128)}), f32[128,1024]{1,0:T(8,128)}) %reduce-scatter.51.cloned.1.call-update) | async-done | bytes 524304 | tf_op jit(solution)/shard_map/reduce_scatter | solution.py:209
  783.8 38.4 %reduce-scatter.53.cloned.1.call-done = f32[1024,128]{1,0:T(8,128)} async-done(((f32[1024,512]{1,0:T(8,128)}), f32[1024,128]{1,0:T(8,128)}) %reduce-scatter.53.cloned.1.call-update) | async-done | bytes 524304 | tf_op jit(solution)/shard_map/reduce_scatter | solution.py:210
  822.2 31.9 %reduce-scatter.37.cloned.1.call-done = f32[384,192]{0,1:T(8,128)} async-done(((f32[384,768]{0,1:T(8,128)}), f32[384,192]{0,1:T(8,128)}) %reduce-scatter.37.cloned.1.call-update) | async-done | bytes 294928 | tf_op jit(solution)/shard_map/reduce_scatter | solution.py:208
  854.1 60.1 %reduce-scatter.39.cloned.1.call-done = f32[192,1536]{1,0:T(8,128)} async-done(((f32[768,1536]{1,0:T(8,128)}), f32[192,1536]{1,0:T(8,128)}) %reduce-scatter.39.cloned.1.call-update) | async-done | bytes 1179664 | tf_op jit(solution)/shard_map/reduce_scatter | solution.py:209
  914.3 60.1 %reduce-scatter.41.cloned.1.call-done = f32[1536,192]{0,1:T(8,128)} async-done(((f32[1536,768]{0,1:T(8,128)}), f32[1536,192]{0,1:T(8,128)}) %reduce-scatter.41.cloned.1.call-update) | async-done | bytes 1179664 | tf_op jit(solution)/shard_map/reduce_scatter | solution.py:210
  974.4 34.0 %reduce-scatter.47.cloned.1.call-done = f32[3,128,256]{2,1,0:T(8,128)} async-done(((f32[3,512,256]{2,1,0:T(8,128)}), f32[3,128,256]{2,1,0:T(8,128)}) %reduce-scatter.47.cloned.1.call-update) | async-done | bytes 393232 | tf_op jit(solution)/shard_map/reduce_scatter | solution.py:207
  1008.3 50.2 %reduce-scatter.35.cloned.1.call-done = f32[3,192,384]{2,1,0:T(8,128)} async-done(((f32[3,768,384]{2,1,0:T(8,128)}), f32[3,192,384]{2,1,0:T(8,128)}) %reduce-scatter.35.cloned.1.call-update) | async-done | bytes 884752 | tf_op jit(solution)/shard_map/reduce_scatter | solution.py:207
  1058.6 29.6 %reduce-scatter.65.cloned.1.call-done = f32[384,1]{1,0:T(8,128)} async-done(((f32[1536,1]{1,0:T(8,128)}), f32[384,1]{1,0:T(8,128)}) %reduce-scatter.65.cloned.1.call-update) | async-done | bytes 1552
  1089.2 30.9 %reduce-scatter.59.cloned.1.call-done = f32[576,1]{1,0:T(8,128)} async-done(((f32[2304,1]{1,0:T(8,128)}), f32[576,1]{1,0:T(8,128)}) %reduce-scatter.59.cloned.1.call-update) | async-done | bytes 2320
  1129.0 18.4 %reduce-scatter.61.cloned.1.call-done = f32[128,2]{1,0:T(8,128)} async-done(((f32[512,2]{1,0:T(8,128)}), f32[128,2]{1,0:T(8,128)}) %reduce-scatter.61.cloned.1.call-update) | async-done | bytes 1040
  1148.3 27.1 %reduce-scatter.55.cloned.1.call-done = f32[192,2]{1,0:T(8,128)} async-done(((f32[768,2]{1,0:T(8,128)}), f32[192,2]{1,0:T(8,128)}) %reduce-scatter.55.cloned.1.call-update) | async-done | bytes 1552
  1176.4 26.7 %reduce-scatter.63.cloned.1.call-done = f32[128,4]{1,0:T(8,128)} async-done(((f32[512,4]{1,0:T(8,128)}), f32[128,4]{1,0:T(8,128)}) %reduce-scatter.63.cloned.1.call-update) | async-done | bytes 2064
  1204.0 26.8 %reduce-scatter.57.cloned.1.call-done = f32[192,4]{1,0:T(8,128)} async-done(((f32[768,4]{1,0:T(8,128)}), f32[192,4]{1,0:T(8,128)}) %reduce-scatter.57.cloned.1.call-update) | async-done | bytes 3088
  1231.7 21.5 %all-reduce.1 = (f32[2,192]{1,0:T(2,128)}, f32[4,192]{1,0:T(4,128)}, f32[1,576]{1,0:T(1,128)}, f32[2,128]{1,0:T(2,128)}, f32[4,128]{1,0:T(4,128)}, /*index=5*/f32[1,384]{1,0:T(1,128)}) all-reduce(f32[2,192]{1,0:T(2,128)S(1)} %copy.101, f32[4,192]{1,0:T(4,128)S(1)} %copy.103, ...), channel_id=1, replica_groups=mesh['fsdp'=4,'ctx'=4,'tp'=2] {'ctx'}, use_global_device_ids=true, to_apply=%region_24.25 | all-reduce | flops 2880 | bytes 23040 | tf_op jit(solution)/shard_map/psum | solution.py:212
  1253.2 167.8 %all-reduce.11.cloned.1.call-done = (f32[3,192,384]{2,1,0:T(8,128)}, f32[384,192]{0,1:T(8,128)}, f32[192,1536]{1,0:T(8,128)}, f32[1536,192]{0,1:T(8,128)}, f32[3...) async-done(((f32[3,192,384]{2,1,0:T(8,128)}, f32[384,192]{0,1:T(8,128)}, f32[192,1536]{1,0:T(8,128)}, f32[1536,192]{0,1:T(8,128)}, ...) | async-done | bytes 5111824 | tf_op jit(solution)/shard_map/psum | solution.py:212
  (542 shorter events, 314.9 us)
Async XLA Ops:
  7.2 42.9 %copy-start.6 = (bf16[1,512,512]{2,1,0:T(8,128)(2,1)S(1)}, bf16[1,512,512]{2,1,0:T(8,128)(2,1)}, u32[]{:S(2)}) copy-start(bf16[1,512,512]{2,1,0:T(8,128)(2,1)} %param.38) | copy-start | bytes 1572868
  7.2 73.8 %all-gather.12.cloned.1.call-start = ((), (), s32[]{:S(2)}) async-start(), calls=%async_computation.18 | async-start | bytes 2211840 | tf_op jit(solution)/shard_map/all_gather | solution.py:46
  7.9 95.5 %all-gather.24.cloned.1.call-start = ((), (), s32[]{:S(2)}) async-start(), calls=%async_computation.30 | async-start | bytes 1310720 | tf_op jit(solution)/shard_map/all_gather | solution.py:88
  50.1 33.6 %copy-start.21 = (bf16[3,512,256]{2,1,0:T(8,128)(2,1)}, bf16[3,512,256]{2,1,0:T(8,128)(2,1)S(1)}, u32[]{:S(2)}) copy-start(bf16[3,512,256]{2,1,0:T(8,128)(2,1)S(1)} %all_gather.65) | copy-start | bytes 2359300
  50.5 18.5 %copy-start.90 = (u32[32]{0:T(128)S(1)}, u32[32]{0:T(128)}, u32[]{:S(2)}) copy-start(u32[32]{0:T(128)} %constant.151) | copy-start | bytes 388
  50.5 19.7 %copy-start.83 = (bf16[1,576]{1,0:T(2,128)(2,1)S(1)}, bf16[1,576]{1,0:T(2,128)(2,1)}, u32[]{:S(2)}) copy-start(bf16[1,576]{1,0:T(2,128)(2,1)} %param.33) | copy-start | bytes 3460
  50.5 29.9 %copy-start.4 = (bf16[1,512,768]{2,1,0:T(8,128)(2,1)S(1)}, bf16[1,512,768]{2,1,0:T(8,128)(2,1)}, u32[]{:S(2)}) copy-start(bf16[1,512,768]{2,1,0:T(8,128)(2,1)} %param.28) | copy-start | bytes 2359300
  51.4 32.3 %copy-start.31 = (bf16[512,512]{1,0:T(8,128)(2,1)}, bf16[512,512]{1,0:T(8,128)(2,1)S(1)}, u32[]{:S(2)}) copy-start(bf16[512,512]{1,0:T(8,128)(2,1)S(1)} %fusion.143) | copy-start | bytes 1572868
  52.4 57.8 %all-gather.22.cloned.1.call-start = ((), (), s32[]{:S(2)}) async-start(), calls=%async_computation.29 | async-start | bytes 1310720 | tf_op jit(solution)/shard_map/all_gather | solution.py:87
  53.5 97.1 %all-gather.16.cloned.1.call-start = ((), (), s32[]{:S(2)}) async-start(), calls=%async_computation.20 | async-start | bytes 1966080 | tf_op jit(solution)/shard_map/all_gather | solution.py:88
  79.8 68.6 %copy-start.56 = (f32[768]{0:T(1024)}, f32[768]{0:T(1024)S(1)}, u32[]{:S(2)}) copy-start(f32[768]{0:T(1024)S(1)} %get-tuple-element.453) | copy-start | bytes 9220
  80.4 68.0 %copy-start.78 = (f32[768]{0:T(1024)}, f32[768]{0:T(1024)S(1)}, u32[]{:S(2)}) copy-start(f32[768]{0:T(1024)S(1)} %get-tuple-element.449) | copy-start | bytes 9220
  80.4 277.1 %copy-start.80 = (f32[768]{0:T(1024)}, f32[768]{0:T(1024)S(1)}, u32[]{:S(2)}) copy-start(f32[768]{0:T(1024)S(1)} %get-tuple-element.447) | copy-start | bytes 9220
  80.6 67.8 %copy-start.62 = (f32[512]{0:T(512)}, f32[512]{0:T(512)S(1)}, u32[]{:S(2)}) copy-start(f32[512]{0:T(512)S(1)} %broadcast_multiply_fusion.11) | copy-start | bytes 6148
  81.0 67.4 %copy-start.64 = (f32[512]{0:T(512)}, f32[512]{0:T(512)S(1)}, u32[]{:S(2)}) copy-start(f32[512]{0:T(512)S(1)} %add_rsqrt_fusion.3) | copy-start | bytes 6148
  83.5 19.8 %copy-start.50 = (s32[1,2048]{1,0:T(1,128)S(1)}, s32[1,2048]{1,0:T(1,128)}, u32[]{:S(2)}) copy-start(s32[1,2048]{1,0:T(1,128)} %param.29) | copy-start | bytes 24580
  83.5 19.9 %copy-start.86 = (s32[1,2048]{1,0:T(1,128)S(1)}, s32[1,2048]{1,0:T(1,128)}, u32[]{:S(2)}) copy-start(s32[1,2048]{1,0:T(1,128)} %param.39) | copy-start | bytes 24580
  83.6 103.2 %all-gather.14.cloned.1.call-start = ((), (), s32[]{:S(2)}) async-start(), calls=%async_computation.19 | async-start | bytes 1966080 | tf_op jit(solution)/shard_map/all_gather | solution.py:87
  93.5 53.6 %copy-start.27 = (bf16[256,512]{1,0:T(8,128)(2,1)}, bf16[256,512]{1,0:T(8,128)(2,1)S(1)}, u32[]{:S(2)}) copy-start(bf16[256,512]{1,0:T(8,128)(2,1)S(1)} %all_gather.69) | copy-start | bytes 786436
  103.3 133.3 %copy-start.16 = (bf16[384,768]{0,1:T(8,128)(2,1)}, bf16[384,768]{0,1:T(8,128)(2,1)S(1)}, u32[]{:S(2)}) copy-start(bf16[384,768]{0,1:T(8,128)(2,1)S(1)} %all_gather.60) | copy-start | bytes 1769476
  116.0 143.6 %all-reduce.17.cloned.1.call-start = ((), (), s32[]{:S(2)}) async-start(), calls=%async_computation.48 | async-start | bytes 5242880 | tf_op jit(solution)/shard_map/psum | solution.py:26
  238.4 51.1 %all-gather.26.cloned.1.call-start = ((), (), s32[]{:S(2)}) async-start(), calls=%async_computation.31 | async-start | bytes 1310720 | tf_op jit(solution)/shard_map/all_gather | solution.py:48
  239.2 78.8 %all-gather.28.cloned.1.call-start = ((), (), s32[]{:S(2)}) async-start(), calls=%async_computation.32 | async-start | bytes 1310720 | tf_op jit(solution)/shard_map/all_gather | solution.py:49
  239.9 117.6 %all-gather.18.cloned.1.call-start = ((), (), s32[]{:S(2)}) async-start(), calls=%async_computation.21 | async-start | bytes 2949120 | tf_op jit(solution)/shard_map/all_gather | solution.py:48
  240.7 156.2 %all-gather.20.cloned.1.call-start = ((), (), s32[]{:S(2)}) async-start(), calls=%async_computation.22 | async-start | bytes 2949120 | tf_op jit(solution)/shard_map/all_gather | solution.py:49
  241.3 187.4 %all-reduce.15.cloned.1.call-start = ((), (), s32[]{:S(2)}) async-start(), calls=%async_computation.47 | async-start | bytes 5242880 | tf_op jit(solution)/shard_map/psum | solution.py:26
  289.5 28.5 %copy-start.29 = (bf16[1,512,512]{2,1,0:T(8,128)(2,1)S(1)}, bf16[1,512,512]{2,1,0:T(8,128)(2,1)}, u32[]{:S(2)}) copy-start(bf16[1,512,512]{2,1,0:T(8,128)(2,1)} %param.40) | copy-start | bytes 1572868
  406.2 147.3 %reduce-scatter.43.cloned.1.call-start = ((), (), s32[]{:S(2)}) async-start(), calls=%async_computation.33 | async-start | bytes 2621440 | tf_op jit(solution)/shard_map/reduce_scatter | solution.py:168
  466.6 90.8 %reduce-scatter.45.cloned.1.call-start = ((), (), s32[]{:S(2)}) async-start(), calls=%async_computation.34 | async-start | bytes 2621440 | tf_op jit(solution)/shard_map/reduce_scatter | solution.py:169
  474.8 144.3 %reduce-scatter.31.cloned.1.call-start = ((), (), s32[]{:S(2)}) async-start(), calls=%async_computation.23 | async-start | bytes 3932160 | tf_op jit(solution)/shard_map/reduce_scatter | solution.py:168
  540.1 141.6 %reduce-scatter.33.cloned.1.call-start = ((), (), s32[]{:S(2)}) async-start(), calls=%async_computation.24 | async-start | bytes 3932160 | tf_op jit(solution)/shard_map/reduce_scatter | solution.py:169
  540.7 192.3 %all-reduce.13.cloned.1.call-start = ((), (), s32[]{:S(2)}) async-start(), calls=%async_computation.46 | async-start | bytes 10485760 | tf_op jit(solution)/shard_map/psum | solution.py:26
  685.7 60.1 %reduce-scatter.49.cloned.1.call-start = ((), (), s32[]{:S(2)}) async-start(), calls=%async_computation.36 | async-start | bytes 655360 | tf_op jit(solution)/shard_map/reduce_scatter | solution.py:208
  689.0 94.8 %reduce-scatter.51.cloned.1.call-start = ((), (), s32[]{:S(2)}) async-start(), calls=%async_computation.37 | async-start | bytes 2621440 | tf_op jit(solution)/shard_map/reduce_scatter | solution.py:209
  692.5 129.7 %reduce-scatter.53.cloned.1.call-start = ((), (), s32[]{:S(2)}) async-start(), calls=%async_computation.38 | async-start | bytes 2621440 | tf_op jit(solution)/shard_map/reduce_scatter | solution.py:210
  697.1 157.1 %reduce-scatter.37.cloned.1.call-start = ((), (), s32[]{:S(2)}) async-start(), calls=%async_computation.26 | async-start | bytes 1474560 | tf_op jit(solution)/shard_map/reduce_scatter | solution.py:208
  700.3 214.0 %reduce-scatter.39.cloned.1.call-start = ((), (), s32[]{:S(2)}) async-start(), calls=%async_computation.27 | async-start | bytes 5898240 | tf_op jit(solution)/shard_map/reduce_scatter | solution.py:209
  705.5 268.9 %reduce-scatter.41.cloned.1.call-start = ((), (), s32[]{:S(2)}) async-start(), calls=%async_computation.28 | async-start | bytes 5898240 | tf_op jit(solution)/shard_map/reduce_scatter | solution.py:210
  713.0 295.4 %reduce-scatter.47.cloned.1.call-start = ((), (), s32[]{:S(2)}) async-start(), calls=%async_computation.35 | async-start | bytes 1966080 | tf_op jit(solution)/shard_map/reduce_scatter | solution.py:207
  718.9 339.6 %reduce-scatter.35.cloned.1.call-start = ((), (), s32[]{:S(2)}) async-start(), calls=%async_computation.25 | async-start | bytes 4423680 | tf_op jit(solution)/shard_map/reduce_scatter | solution.py:207
  725.3 362.9 %reduce-scatter.65.cloned.1.call-start = ((), (), s32[]{:S(2)}) async-start(), calls=%async_computation.44 | async-start | bytes 983040
  730.1 390.0 %reduce-scatter.59.cloned.1.call-start = ((), (), s32[]{:S(2)}) async-start(), calls=%async_computation.41 | async-start | bytes 1474560
  732.9 414.5 %reduce-scatter.61.cloned.1.call-start = ((), (), s32[]{:S(2)}) async-start(), calls=%async_computation.42 | async-start | bytes 327680
  736.8 438.6 %reduce-scatter.55.cloned.1.call-start = ((), (), s32[]{:S(2)}) async-start(), calls=%async_computation.39 | async-start | bytes 491520
  737.8 465.2 %reduce-scatter.63.cloned.1.call-start = ((), (), s32[]{:S(2)}) async-start(), calls=%async_computation.43 | async-start | bytes 327680
  738.8 491.9 %reduce-scatter.57.cloned.1.call-start = ((), (), s32[]{:S(2)}) async-start(), calls=%async_computation.40 | async-start | bytes 491520
  739.9 681.1 %all-reduce.11.cloned.1.call-start = ((), (), s32[]{:S(2)}) async-start(), calls=%async_computation.45 | async-start | bytes 10223616 | tf_op jit(solution)/shard_map/psum | solution.py:212
  1058.5 62.7 %copy-start.77 = (f32[1,512]{1,0:T(1,128)S(1)}, f32[1,512]{1,0:T(1,128)}, u32[]{:S(2)}) copy-start(f32[1,512]{1,0:T(1,128)} %get-tuple-element.576) | copy-start | bytes 6148
  (89 other events, 236.1 us)
Sparse Core Ops, SparseCore 0:
  9.9 39.6 all-gather.11
  52.6 27.9 all-gather.23
  82.7 27.4 all-gather.21
  112.2 36.5 all-gather.15
  150.8 35.9 all-gather.13
  238.5 21.0 all-reduce.16
  261.6 27.8 all-gather.25
  291.5 26.4 all-gather.27
  320.0 37.4 all-gather.17
  359.3 37.4 all-gather.19
  406.3 22.2 all-reduce.14
  466.7 45.0 reduce-scatter.42
  514.2 43.1 reduce-scatter.44
  559.5 59.5 reduce-scatter.30
  621.3 60.2 reduce-scatter.32
  685.8 30.3 all-reduce.12
  719.7 26.0 reduce-scatter.48
  748.6 35.1 reduce-scatter.50
  787.0 35.1 reduce-scatter.52
  825.6 28.5 reduce-scatter.36
  857.1 57.0 reduce-scatter.38
  917.2 57.0 reduce-scatter.40
  977.4 30.9 reduce-scatter.46
  1011.3 47.2 reduce-scatter.34
  1062.0 26.1 reduce-scatter.64
  1091.5 28.4 reduce-scatter.58
  1123.2 24.0 reduce-scatter.60
  1151.0 24.4 reduce-scatter.54
  1179.0 24.0 reduce-scatter.62
  1206.3 24.4 reduce-scatter.56
  1233.7 187.2 all-reduce.10
where the time goes:
time: 1450 us; the launch traced here: 1440 us
  waiting for transfers between devices  962 us (66%)
  matrix products  238 us (16%)
  blocking collectives  105 us (7%)
  local copies, waits for them, and re-layouts  70.3 us (5%)
  other arithmetic  41.6 us (3%)
  between operations  16.9 us (1%)
    psum x1, waiting for transfers between devices, run_block(): lax.psum((share_gains, share_shifts, share_head, share_qkv, share_proj, s...  168 us
    unnamed x37, waiting for transfers between devices  164 us
    reduce_scatter x2, waiting for transfers between devices, run_block(): lax.psum_scatter(grad_down, 'fsdp', scatter_dimension=1, tiled=True)  98.6 us
    reduce_scatter x2, waiting for transfers between devices, run_block(): lax.psum_scatter(grad_up, 'fsdp', scatter_dimension=0, tiled=True)  98.2 us
    reduce_scatter x2, waiting for transfers between devices, run_block(): lax.psum_scatter(grad_qkv, 'fsdp', scatter_dimension=1, tiled=True)  84.1 us
    reduce_scatter x2, waiting for transfers between devices, run_block(): lax.psum_scatter(from_heads(value_parts), 'ctx', scatter_dimension=0, til...  60.6 us
    all_gather x2, waiting for transfers between devices, run_block(): lax.all_gather(up_weight, 'fsdp', axis=0, tiled=True)  60.4 us
    all_gather x2, waiting for transfers between devices, run_block(): lax.all_gather(down_weight, 'fsdp', axis=1, tiled=True)  59.1 us
  transfers between devices with their start and end apart: 31, of which 26 were waited for; matrix products, arithmetic and copies ran while one was open for 16% of the time, Pallas kernels for 0%

commit v1 on v0

--- a/solution.py
+++ b/solution.py
@@ -1,9 +1,364 @@
+import functools
+
 import jax
 import jax.numpy as jnp
 from jax import lax
+from jax.experimental import pallas as pl
+from jax.experimental.pallas import tpu as pltpu
 from jax.sharding import PartitionSpec as P
 
 HD = 64
+LANES = 128
+QB = 256
+KB = 512
+NEG = -1e30
+F32 = jnp.float32
+BF16 = jnp.bfloat16
+ACROSS_X = [(i, i ^ 1) for i in range(4)]
+ACROSS_Y = [(i, i ^ 2) for i in range(4)]
+
+
+def dot(left, right, dims=((1,), (0,))):
+    return lax.dot_general(left, right, (dims, ((), ())), preferred_element_type=F32)
+
+
+def gather_rows(piece):
+    group = lax.axis_index("fsdp")
+    rows = piece.shape[0]
+    half = rows // 2
+    from_x = lax.ppermute(piece, "fsdp", ACROSS_X)
+    from_y = lax.ppermute(piece, "fsdp", ACROSS_Y)
+    far_top = lax.ppermute(from_y[:half], "fsdp", ACROSS_X)
+    far_low = lax.ppermute(from_x[half:], "fsdp", ACROSS_Y)
+    whole = jnp.zeros((4 * rows,) + piece.shape[1:], piece.dtype)
+
+    def put(whole, part, owner, offset=0):
+        return lax.dynamic_update_slice_in_dim(whole, part, owner * rows + offset, 0)
+
+    whole = put(whole, piece, group)
+    whole = put(whole, from_x, group ^ 1)
+    whole = put(whole, from_y, group ^ 2)
+    whole = put(whole, far_top, group ^ 3)
+    return put(whole, far_low, group ^ 3, half)
+
+
+def swap_blocks(blocks):
+    here = lax.axis_index("ctx")
+
+    def pick(index):
+        return lax.dynamic_index_in_dim(blocks, index, 0, keepdims=True)
+
+    out = jnp.zeros_like(blocks)
+    out = lax.dynamic_update_slice_in_dim(out, pick(here), here, 0)
+    for step in (1, 2, 3):
+        pairs = [(i, i ^ step) for i in range(4)]
+        out = lax.dynamic_update_slice_in_dim(
+            out, lax.ppermute(pick(here ^ step), "ctx", pairs), here ^ step, 0
+        )
+    return out
+
+
+def other_core(rows):
+    return lax.ppermute(rows, "tp", [(0, 1), (1, 0)])
+
+
+def tensor_sum(rows):
+    return rows + other_core(rows)
+
+
+def reduce_owned(partial):
+    group = lax.axis_index("fsdp")
+    here = lax.axis_index("ctx")
+    rows = partial.shape[0] // 4
+    half = rows // 2
+    low = partial.astype(BF16)
+
+    def take(array, owner, offset):
+        return lax.dynamic_slice_in_dim(array, owner * rows + offset, half, 0)
+
+    def pair(owner_one, owner_two, offset):
+        return jnp.concatenate([take(low, owner_one, offset), take(low, owner_two, offset)])
+
+    top = lax.ppermute(pair(group ^ 1, group ^ 3, 0), "fsdp", ACROSS_X).astype(F32)
+    bottom = lax.ppermute(pair(group ^ 2, group ^ 3, half), "fsdp", ACROSS_Y).astype(F32)
+    top_pass = (take(partial, group ^ 2, 0).astype(F32) + top[half:]).astype(BF16)
+    low_pass = (take(partial, group ^ 1, half).astype(F32) + bottom[half:]).astype(BF16)
+    top_back = lax.ppermute(top_pass, "fsdp", ACROSS_Y).astype(F32)
+    low_back = lax.ppermute(low_pass, "fsdp", ACROSS_X).astype(F32)
+    top_sum = take(partial, group, 0).astype(F32) + top[:half] + top_back
+    low_sum = take(partial, group, half).astype(F32) + bottom[:half] + low_back
+    owned = jnp.concatenate([top_sum, low_sum])
+    quarter = rows // 4
+    owned_low = owned.astype(BF16)
+
+    def cut(array, index):
+        return lax.dynamic_slice_in_dim(array, index * quarter, quarter, 0)
+
+    total = cut(owned, here)
+    for step in (1, 2, 3):
+        pairs = [(i, i ^ step) for i in range(4)]
+        total = total + lax.ppermute(cut(owned_low, here ^ step), "ctx", pairs).astype(F32)
+    total = total.astype(BF16)
+    out = jnp.zeros((4, quarter, partial.shape[1]), BF16)
+    out = lax.dynamic_update_slice_in_dim(out, total[None], here, 0)
+    for step in (1, 2, 3):
+        pairs = [(i, i ^ step) for i in range(4)]
+        out = lax.dynamic_update_slice_in_dim(
+            out, lax.ppermute(total, "ctx", pairs)[None], here ^ step, 0
+        )
+    return out.reshape(rows, partial.shape[1]).astype(F32)
+
+
+def reduce_small(vector):
+    for axis, pairs in (
+        ("fsdp", ACROSS_X),
+        ("fsdp", ACROSS_Y),
+        ("ctx", [(i, i ^ 1) for i in range(4)]),
+        ("ctx", [(i, i ^ 2) for i in range(4)]),
+    ):
+        vector = vector + lax.ppermute(vector, axis, pairs)
+    return vector
+
+
+def lane_marks():
+    lane = lax.broadcasted_iota(jnp.int32, (1, LANES), 1)
+    first = (lane < HD).astype(F32).astype(BF16)
+    second = (lane >= HD).astype(F32).astype(BF16)
+    return first, second
+
+
+def attend_kernel(
+    causal, bounds, q_ref, kv_ref, extra_ref, segcol_ref, segrow_ref, o_ref, lse_ref
+):
+    block = pl.program_id(0)
+    low, high, active = bounds[0, block], bounds[1, block], bounds[2, block]
+    first, second = lane_marks()
+    lane = lax.broadcasted_iota(jnp.int32, (QB, LANES), 1)
+    query = q_ref[...]
+    seg_query = segcol_ref[...]
+
+    def one(query, keys_ref, own, other):
+        def step(index, carry):
+            top, acc = carry
+            start = pl.multiple_of(index * KB, KB)
+            keys = keys_ref[pl.ds(start, KB), :]
+            scores = dot(query * own, keys, ((1,), (1,)))
+            ok = seg_query == segrow_ref[:, pl.ds(start, KB)]
+            if causal:
+                key_pos = start + lax.broadcasted_iota(jnp.int32, (QB, KB), 1)
+                query_pos = block * QB + lax.broadcasted_iota(jnp.int32, (QB, KB), 0)
+                ok = jnp.logical_and(ok, key_pos <= query_pos)
+            scores = jnp.where(ok, scores, NEG)
+            new_top = jnp.maximum(top, jnp.max(scores, axis=1, keepdims=True))
+            weights = jnp.exp(scores - new_top).astype(BF16)
+            acc = acc * jnp.exp(top - new_top) + dot(weights, keys * other + own)
+            return new_top, acc
+
+        top, acc = lax.fori_loop(
+            low, high, step, (jnp.full((QB, 1), NEG, F32), jnp.zeros((QB, LANES), F32))
+        )
+        return acc / pltpu.roll(acc, HD, 1), top + jnp.log(acc)
+
+    mixed, lse = one(query, kv_ref, first, second)
+    if extra_ref is None:
+        o_ref[...] = mixed.astype(BF16)
+        lse_ref[0] = jnp.transpose(lse)[:16]
+    else:
+
+        @pl.when(active == 0)
+        def _():
+            o_ref[...] = mixed.astype(BF16)
+            lse_ref[0, :8] = jnp.transpose(lse)[:8]
+            lse_ref[0, 8:] = jnp.zeros((8, QB), F32)
+
+        @pl.when(active != 0)
+        def _():
+            mixed_two, lse_two = one(query, extra_ref, second, first)
+            o_ref[...] = jnp.where(lane < HD, mixed_two, mixed).astype(BF16)
+            lse_ref[0, :8] = jnp.transpose(lse)[:8]
+            lse_ref[0, 8:] = jnp.transpose(lse_two)[HD : HD + 8]
+
+
+def attend(causal, bounds, q, kv, extra, segcol, segrow):
+    rows = q.shape[0]
+    body = functools.partial(attend_kernel, causal)
+    if extra is None:
+
+        def kernel(bounds, q_ref, kv_ref, *rest):
+            body(bounds, q_ref, kv_ref, None, *rest)
+
+        wide = [kv]
+    else:
+        kernel = body
+        wide = [kv, extra]
+    whole = pl.BlockSpec((rows, LANES), lambda i, b: (0, 0))
+    block = pl.BlockSpec((QB, LANES), lambda i, b: (i, 0))
+    blocks = rows // QB
+    heads = len(wide)
+    return pl.pallas_call(
+        kernel,
+        grid_spec=pltpu.PrefetchScalarGridSpec(
+            num_scalar_prefetch=1,
+            grid=(blocks,),
+            in_specs=[block]
+            + [whole] * heads
+            + [
+                pl.BlockSpec((QB, 1), lambda i, b: (i, 0)),
+                pl.BlockSpec((1, rows), lambda i, b: (0, 0)),
+            ],
+            out_specs=[block, pl.BlockSpec((1, 16, QB), lambda i, b: (i, 0, 0))],
+        ),
+        out_shape=[
+            jax.ShapeDtypeStruct((rows, LANES), BF16),
+            jax.ShapeDtypeStruct((blocks, 16, QB), F32),
+        ],
+        cost_estimate=pl.CostEstimate(
+            flops=heads * 4 * rows * rows * LANES, bytes_accessed=6 * rows * LANES, transcendentals=heads * rows * rows
+        ),
+        name="attend_causal" if causal else "attend_full",
+    )(bounds, q, *wide, segcol, segrow)
+
+
+def attend_back_kernel(
+    causal,
+    bounds,
+    q_ref,
+    do_ref,
+    o_ref,
+    lse_ref,
+    kv_ref,
+    extra_ref,
+    segcol_ref,
+    segrow_ref,
+    dq_ref,
+    dkv_ref,
+    dextra_ref,
+    acc_ref,
+    acc_extra_ref,
+):
+    block = pl.program_id(0)
+    low, high, active = bounds[0, block], bounds[1, block], bounds[2, block]
+    first, second = lane_marks()
+    lane = lax.broadcasted_iota(jnp.int32, (QB, LANES), 1)
+
+    @pl.when(block == 0)
+    def _():
+        acc_ref[...] = jnp.zeros_like(acc_ref)
+        if acc_extra_ref is not None:
+            acc_extra_ref[...] = jnp.zeros_like(acc_extra_ref)
+
+    query = q_ref[...]
+    grad_o = do_ref[...]
+    product = jnp.transpose(grad_o.astype(F32) * o_ref[...].astype(F32))
+    seg_query = segrow_ref[:, pl.ds(pl.multiple_of(block * QB, QB), QB)]
+
+    def one(keys_ref, total_ref, own, other, lse, delta):
+        query_own = query * own
+        grad_own = grad_o * other
+
+        def step(index, grad_query):
+            start = pl.multiple_of(index * KB, KB)
+            keys = keys_ref[pl.ds(start, KB), :]
+            scores = dot(keys, query_own, ((1,), (1,)))
+            ok = segcol_ref[pl.ds(start, KB), :] == seg_query
+            if causal:
+                key_pos = start + lax.broadcasted_iota(jnp.int32, (KB, QB), 0)
+                query_pos = block * QB + lax.broadcasted_iota(jnp.int32, (KB, QB), 1)
+                ok = jnp.logical_and(ok, key_pos <= query_pos)
+            weights = jnp.where(ok, jnp.exp(scores - lse), 0.0)
+            grad_weights = dot(keys, grad_own, ((1,), (1,)))
+            grad_scores = (weights * (grad_weights - delta)).astype(BF16)
+            total_ref[pl.ds(start, KB), :] += dot(grad_scores, query_own) + dot(
+                weights.astype(BF16), grad_own
+            )
+            return grad_query + dot(grad_scores, keys, ((0,), (0,)))
+
+        return lax.fori_loop(low, high, step, jnp.zeros((QB, LANES), F32))
+
+    grad_query = one(
+        kv_ref,
+        acc_ref,
+        first,
+        second,
+        lse_ref[0, :1],
+        jnp.sum(product[HD:], axis=0, keepdims=True),
+    )
+    if extra_ref is None:
+        dq_ref[...] = (grad_query * 0.125).astype(BF16)
+    else:
+
+        @pl.when(active == 0)
+        def _():
+            dq_ref[...] = (grad_query * 0.125).astype(BF16)
+
+        @pl.when(active != 0)
+        def _():
+            grad_two = one(
+                extra_ref,
+                acc_extra_ref,
+                second,
+                first,
+                lse_ref[0, 8:9],
+                jnp.sum(product[:HD], axis=0, keepdims=True),
+            )
+            dq_ref[...] = (jnp.where(lane < HD, grad_query, grad_two) * 0.125).astype(BF16)
+
+    @pl.when(block == pl.num_programs(0) - 1)
+    def _():
+        dkv_ref[...] = acc_ref[...].astype(BF16)
+        if dextra_ref is not None:
+            dextra_ref[...] = acc_extra_ref[...].astype(BF16)
+
+
+def attend_back(causal, bounds, q, do, o, lse, kv, extra, segcol, segrow):
+    rows = q.shape[0]
+    body = functools.partial(attend_back_kernel, causal)
+    if extra is None:
+
+        def kernel(bounds, q, do, o, lse, kv, sc, sr, dq, dkv, acc):
+            body(bounds, q, do, o, lse, kv, None, sc, sr, dq, dkv, None, acc, None)
+
+        wide = [kv]
+    else:
+        kernel = body
+        wide = [kv, extra]
+    whole = pl.BlockSpec((rows, LANES), lambda i, b: (0, 0))
+    block = pl.BlockSpec((QB, LANES), lambda i, b: (i, 0))
+    blocks = rows // QB
+    heads = len(wide)
+    return pl.pallas_call(
+        kernel,
+        grid_spec=pltpu.PrefetchScalarGridSpec(
+            num_scalar_prefetch=1,
+            grid=(blocks,),
+            in_specs=[block] * 3
+            + [pl.BlockSpec((1, 16, QB), lambda i, b: (i, 0, 0))]
+            + [whole] * heads
+            + [
+                pl.BlockSpec((rows, 1), lambda i, b: (0, 0)),
+                pl.BlockSpec((1, rows), lambda i, b: (0, 0)),
+            ],
+            out_specs=[block] + [whole] * heads,
+            scratch_shapes=[pltpu.VMEM((rows, LANES), F32)] * heads,
+        ),
+        out_shape=[jax.ShapeDtypeStruct((rows, LANES), BF16)] * (1 + heads),
+        cost_estimate=pl.CostEstimate(
+            flops=heads * 10 * rows * rows * LANES, bytes_accessed=12 * rows * LANES, transcendentals=heads * rows * rows
+        ),
+        name="attend_back_causal" if causal else "attend_back_full",
+    )(bounds, q, do, o, lse, *wide, segcol, segrow)
+
+
+def block_bounds(seg, causal):
+    blocks = seg.reshape(-1, QB)
+    begin = jnp.sum(seg[None, :] < blocks[:, :1], axis=1, dtype=jnp.int32)
+    end = jnp.sum(seg[None, :] <= blocks[:, -1:], axis=1, dtype=jnp.int32)
+    if causal:
+        end = jnp.minimum(end, (jnp.arange(blocks.shape[0], dtype=jnp.int32) + 1) * QB)
+    half = lax.axis_index("ctx") % 2
+    count = blocks.shape[0]
+    active = (jnp.arange(count, dtype=jnp.int32) // (count // 2) == half).astype(jnp.int32)
+    return jnp.stack([begin // KB, (end + KB - 1) // KB, active])
 
 
 def layer_stats(rows):
@@ -22,11 +377,304 @@
     )
 
 
-def tensor_sum(partial_rows):
+def head(array, index):
+    return array[:, index * HD : (index + 1) * HD]
+
+
+def gather_first(gains, shifts, head_bias, qkv_weight):
+    rows, columns = qkv_weight.shape[1], 3 * qkv_weight.shape[2]
+    weight = qkv_weight.transpose(1, 0, 2).reshape(rows, columns)
+    small = jnp.concatenate([gains.reshape(-1), shifts.reshape(-1), head_bias.reshape(-1)])
+    small = jnp.pad(small, (0, 16 * columns - small.size)).reshape(16, columns)
+    whole = gather_rows(jnp.concatenate([weight, small])).reshape(4, rows + 16, columns)
+    small = whole[:, rows:].reshape(4, -1)
+    g, s = gains.size, shifts.size
+    gain_vals = small[:, :g].reshape(4, 2, rows).transpose(1, 0, 2).reshape(2, -1)
+    shift_vals = small[:, g : g + s].reshape(4, 4, rows).transpose(1, 0, 2).reshape(4, -1)
+    bias_vals = small[:, g + s : g + s + head_bias.size].reshape(-1)
+    return (
+        whole[:, :rows].reshape(4 * rows, columns),
+        gain_vals.astype(F32),
+        shift_vals.astype(F32),
+        bias_vals.astype(F32),
+    )
+
+
+def forward_first(rows_in, params, weight_first, heads):
+    gain_vals, shift_vals, bias_vals = params
+    rows = rows_in[0].astype(F32)
+    width = heads * HD
+    normed, inv = layer_stats(rows)
+    first_in = (normed * gain_vals[0] + shift_vals[0]).astype(BF16)
+    qkv = dot(first_in, weight_first)
+    q = (qkv[:, :width] + bias_vals[:width]).astype(BF16) * jnp.asarray(0.125, BF16)
+    k = qkv[:, width : 2 * width].astype(BF16)
+    v = (qkv[:, 2 * width :] + bias_vals[width : 2 * width]).astype(BF16)
+    return first_in, q, k, v
+
+
+def pack_qkv(q, k, v, heads):
+    out = []
+    for c in range(4):
+        if heads == 4:
+            parts = [(head(q, c), jnp.zeros_like(head(q, c))), (head(k, c), head(v, c))]
+        else:
+            e = 4 + c // 2
+            parts = [
+                (head(q, c), head(q, e)),
+                (head(k, c), head(v, c)),
+                (head(v, e), head(k, e)),
+            ]
+        out.append(jnp.stack([jnp.concatenate(p, axis=1) for p in parts]))
+    return jnp.stack(out)
+
+
+def unpack_o(blocks, heads):
+    columns = [blocks[c][:, HD:] for c in range(4)]
+    if heads == 6:
+        part = lax.axis_index("ctx") // 2
+        for h in range(2):
+            columns.append(
+                lax.dynamic_index_in_dim(blocks[2 * h : 2 * h + 2], part, 0, keepdims=False)[:, :HD]
+            )
+    return jnp.concatenate(columns, axis=1)
+
+
+def pack_do(do, heads):
+    out = []
+    for c in range(4):
+        other = jnp.zeros_like(head(do, c)) if heads == 4 else head(do, 4 + c // 2)
+        out.append(jnp.concatenate([other, head(do, c)], axis=1))
+    return jnp.stack(out)
+
+
+def unpack_dqkv(blocks, heads):
+    dq = [blocks[c, 0][:, :HD] for c in range(4)]
+    dk = [blocks[c, 1][:, :HD] for c in range(4)]
+    dv = [blocks[c, 1][:, HD:] for c in range(4)]
+    if heads == 6:
+        part = lax.axis_index("ctx") // 2
+        for h in range(2):
+            dq.append(
+                lax.dynamic_index_in_dim(blocks[2 * h : 2 * h + 2, 0], part, 0, keepdims=False)[:, HD:]
+            )
+            both = (
+                blocks[2 * h, 2].astype(F32) + blocks[2 * h + 1, 2].astype(F32)
+            ).astype(BF16)
+            dk.append(both[:, HD:])
+            dv.append(both[:, :HD])
+    return (
+        jnp.concatenate(dq, axis=1),
+        jnp.concatenate(dk, axis=1),
+        jnp.concatenate(dv, axis=1),
+    )
+
+
+def blocks_of(array):
+    return array.reshape(4, -1, array.shape[-1])
+
+
+def middle_part(rows_in, cotangent, mixed, params, rest, heads):
+    gain_vals, shift_vals, bias_vals = params
+    width = heads * HD
+    hidden_width = bias_vals.shape[0] - 2 * width
+    up = rest[:, :hidden_width]
+    down_t = rest[:, hidden_width : 2 * hidden_width]
+    proj_t = rest[:, 2 * hidden_width :]
+    rows = rows_in[0].astype(F32)
+    grad_out = cotangent[0].astype(F32)
+    middle = rows + tensor_sum(dot(mixed, proj_t, ((1,), (1,)))) + shift_vals[1]
+    normed_two, inv_two = layer_stats(middle)
+    second_in = (normed_two * gain_vals[1] + shift_vals[2]).astype(BF16)
+    hidden = dot(second_in, up) + bias_vals[2 * width :]
+    sigma = jax.nn.sigmoid(1.702 * hidden)
+    activated = (hidden * sigma).astype(BF16)
+    grad_branch = cotangent[0]
+    grad_act = dot(grad_branch, down_t)
+    grad_hidden = (grad_act * (sigma + 1.702 * hidden * sigma * (1.0 - sigma))).astype(BF16)
+    grad_second = tensor_sum(dot(grad_hidden, up, ((1,), (1,))))
+    output = (
+        middle + tensor_sum(dot(activated, down_t, ((1,), (1,)))) + shift_vals[3]
+    ).astype(BF16)
+    grad_middle = grad_out + norm_back(grad_second, normed_two, inv_two, gain_vals[1])
+    grad_attn = grad_middle.astype(BF16)
+    grad_mixed = dot(grad_attn, proj_t).astype(BF16)
+    over_rows = ((0,), (0,))
+    grad_rest = jnp.concatenate(
+        [
+            dot(second_in, grad_hidden, over_rows).astype(BF16),
+            dot(grad_branch, activated, over_rows).astype(BF16),
+            dot(grad_attn, mixed, over_rows).astype(BF16),
+        ],
+        axis=1,
+    )
+    small = (
+        jnp.sum(grad_second * normed_two, axis=0),
+        jnp.sum(grad_middle, axis=0),
+        jnp.sum(grad_second, axis=0),
+        jnp.sum(grad_out, axis=0),
+        jnp.sum(grad_hidden.astype(F32), axis=0),
+    )
+    return output, grad_middle, grad_mixed, grad_rest, small
+
+
+def last_part(rows_in, params, weight_first, first_in, dq, dk, dv, grad_middle):
+    gain_vals = params[0]
+    dqkv = jnp.concatenate([dq, dk, dv], axis=1)
+    grad_first = tensor_sum(dot(dqkv, weight_first, ((1,), (1,))))
+    grad_weight = dot(first_in, dqkv, ((0,), (0,))).astype(BF16)
+    normed, inv = layer_stats(rows_in[0].astype(F32))
+    grad_rows = grad_middle + norm_back(grad_first, normed, inv, gain_vals[0])
+    small = (
+        jnp.sum(grad_first * normed, axis=0),
+        jnp.sum(grad_first, axis=0),
+        jnp.sum(dq.astype(F32), axis=0),
+        jnp.sum(dv.astype(F32), axis=0),
+    )
+    return grad_rows, grad_weight, small
+
+
+class Stream:
+    def __init__(self, args, causal):
+        (
+            self.rows_in,
+            seg_row,
+            self.cotangent,
+            gains,
+            shifts,
+            head_bias,
+            qkv_weight,
+            proj_weight,
+            up_weight,
+            down_weight,
+        ) = args
+        self.causal = causal
+        self.heads = qkv_weight.shape[2] // HD
+        self.segrow = seg_row
+        self.segcol = seg_row.reshape(-1, 1)
+        self.bounds = block_bounds(seg_row[0], causal)
+        self.first = (gains, shifts, head_bias, qkv_weight)
+        self.rest = jnp.concatenate(
+            [up_weight, down_weight.T, proj_weight.T], axis=1
+        )
+
+    def gather_first(self):
+        weight, *params = gather_first(*self.first)
+        self.weight_first, self.params = weight, params
+
+    def qkv(self):
+        self.first_in, q, k, v = forward_first(
+            self.rows_in, self.params, self.weight_first, self.heads
+        )
+        got = swap_blocks(pack_qkv(q, k, v, self.heads))
+        parts = [got[:, i].reshape(-1, LANES) for i in range(got.shape[1])]
+        self.q, self.kv = parts[0], parts[1]
+        self.extra = parts[2] if self.heads == 6 else None
+
+    def gather_rest(self):
+        self.rest_full = gather_rows(self.rest)
+
+    def attend(self):
+        self.o, self.lse = attend(
+            self.causal, self.bounds, self.q, self.kv, self.extra, self.segcol, self.segrow
+        )
+        self.mixed = unpack_o(swap_blocks(blocks_of(self.o)), self.heads)
+
+    def middle(self):
+        self.output, self.grad_middle, grad_mixed, self.grad_rest, self.small = middle_part(
+            self.rows_in, self.cotangent, self.mixed, self.params, self.rest_full, self.heads
+        )
+        self.do = swap_blocks(pack_do(grad_mixed, self.heads)).reshape(-1, LANES)
+
+    def back(self):
+        grads = attend_back(
+            self.causal,
+            self.bounds,
+            self.q,
+            self.do,
+            self.o,
+            self.lse,
+            self.kv,
+            self.extra,
+            self.segcol,
+            self.segrow,
+        )
+        got = swap_blocks(jnp.stack([blocks_of(g) for g in grads], axis=1))
+        self.dqkv = unpack_dqkv(got, self.heads)
+
+    def last(self):
+        self.grad_rows, self.grad_first, self.small_last = last_part(
+            self.rows_in,
+            self.params,
+            self.weight_first,
+            self.first_in,
+            *self.dqkv,
+            self.grad_middle,
+        )
+
+    def small_vector(self):
+        gain_two, shift_proj, shift_two, shift_down, bias_up = self.small
+        gain_one, shift_one, bias_q, bias_v = self.small_last
+        return jnp.concatenate(
+            [
+                gain_one,
+                gain_two,
+                shift_one,
+                shift_proj,
+                shift_two,
+                shift_down,
+                bias_q,
+                bias_v,
+                bias_up,
+            ]
+        )
+
+    def outputs(self, small):
+        group = lax.axis_index("fsdp")
+        full = self.rows_in.shape[2]
+        width = self.heads * HD
+        hidden = (self.rest.shape[1] - width) // 2
+
+        def own(array):
+            columns = array.shape[1] // 4
+            return lax.dynamic_slice_in_dim(array, group * columns, columns, 1)
+
+        gains = own(small[: 2 * full].reshape(2, full))
+        shifts = own(small[2 * full : 6 * full].reshape(4, full))
+        bias = own(small[6 * full :].reshape(1, -1))
+        rest = reduce_owned(self.grad_rest)
+        first = reduce_owned(self.grad_first)
+        rows = first.shape[0]
+        return (
+            self.output[None],
+            self.grad_rows[None],
+            gains,
+            shifts,
+            bias,
+            first.reshape(rows, 3, width).transpose(1, 0, 2),
+            rest[:, 2 * hidden :].T,
+            rest[:, :hidden],
+            rest[:, hidden : 2 * hidden].T,
+        )
+
+
+def on_device(*args):
+    image = Stream(args[:10], False)
+    text = Stream(args[10:], True)
+    for stage in ("gather_first", "qkv", "gather_rest", "attend", "middle", "back", "last"):
+        for stream in (text, image):
+            getattr(stream, stage)()
+    small_image, small_text = image.small_vector(), text.small_vector()
+    small = reduce_small(jnp.concatenate([small_image, small_text]))
+    cut = small_image.shape[0]
+    return image.outputs(small[:cut]) + text.outputs(small[cut:])
+
+
+def tensor_psum(partial_rows):
     return lax.psum(partial_rows, "tp")
 
 
-def run_block(
+def any_mesh_block(
     rows_in,
     seg_row,
     cotangent,
@@ -106,7 +754,7 @@
     mixed = from_heads(mixed_heads)
     middle = (
         rows
-        + tensor_sum(jnp.dot(mixed, proj_full, preferred_element_type=jnp.float32))
+        + tensor_psum(jnp.dot(mixed, proj_full, preferred_element_type=jnp.float32))
         + shift_vals[1]
     )
     normed_two, inv_two = layer_stats(middle)
@@ -118,7 +766,7 @@
     activated = (hidden * sigma).astype(jnp.bfloat16)
     output = (
         middle
-        + tensor_sum(jnp.dot(activated, down_full, preferred_element_type=jnp.float32))
+        + tensor_psum(jnp.dot(activated, down_full, preferred_element_type=jnp.float32))
         + shift_vals[3]
     )
     grad_out = cotangent[0].astype(jnp.float32)
@@ -129,7 +777,7 @@
     grad_hidden = (grad_act * (sigma + 1.702 * hidden * sigma * (1.0 - sigma))).astype(jnp.bfloat16)
     grad_up_bias = jnp.sum(grad_hidden.astype(jnp.float32), axis=0)
     grad_up = jnp.einsum("td,tf->df", second_in, grad_hidden, preferred_element_type=jnp.float32)
-    grad_second = tensor_sum(
+    grad_second = tensor_psum(
         jnp.einsum("tf,df->td", grad_hidden, up_full, preferred_element_type=jnp.float32)
     )
     grad_gain_two = jnp.sum(grad_second * normed_two, axis=0)
@@ -194,7 +842,7 @@
     grad_first_part = grad_first_part + jnp.einsum(
         "tc,dc->td", grad_value, qkv_full[2], preferred_element_type=jnp.float32
     )
-    grad_first = tensor_sum(grad_first_part)
+    grad_first = tensor_psum(grad_first_part)
     grad_gain_one = jnp.sum(grad_first * normed_one, axis=0)
     grad_shift_one = jnp.sum(grad_first, axis=0)
     grad_rows = grad_middle + norm_back(grad_first, normed_one, inv_one, gain_vals[0])
@@ -215,7 +863,7 @@
     return (output.astype(jnp.bfloat16)[None], grad_rows[None]) + tuple(owned)
 
 
-def on_device(
+def on_any_mesh(
     image_input,
     image_segments,
     image_cotangent,
@@ -237,7 +885,7 @@
     text_up_weight,
     text_down_weight,
 ):
-    image_results = run_block(
+    image_results = any_mesh_block(
         image_input,
         image_segments,
         image_cotangent,
@@ -250,7 +898,7 @@
         image_down_weight,
         False,
     )
-    text_results = run_block(
+    text_results = any_mesh_block(
         text_input,
         text_segments,
         text_cotangent,
@@ -266,51 +914,27 @@
     return image_results + text_results
 
 
+def stream_specs():
+    return (
+        P("fsdp", "ctx", None),
+        P("fsdp", None),
+        P("fsdp", "ctx", None),
+        P(None, "fsdp"),
+        P(None, "fsdp"),
+        P("tp", "fsdp"),
+        P(None, "fsdp", "tp"),
+        P("tp", "fsdp"),
+        P("fsdp", "tp"),
+        P("tp", "fsdp"),
+    )
+
+
 def solution(mesh):
+    one = stream_specs()
+    grads = (one[0], one[0]) + one[3:]
+    body = on_device
+    if (mesh.shape["fsdp"], mesh.shape["ctx"], mesh.shape["tp"]) != (4, 4, 2):
+        body = on_any_mesh
     return jax.shard_map(
-        on_device,
-        mesh=mesh,
-        in_specs=(
-            P("fsdp", "ctx", None),
-            P("fsdp", None),
-            P("fsdp", "ctx", None),
-            P(None, "fsdp"),
-            P(None, "fsdp"),
-            P("tp", "fsdp"),
-            P(None, "fsdp", "tp"),
-            P("tp", "fsdp"),
-            P("fsdp", "tp"),
-            P("tp", "fsdp"),
-            P("fsdp", "ctx", None),
-            P("fsdp", None),
-            P("fsdp", "ctx", None),
-            P(None, "fsdp"),
-            P(None, "fsdp"),
-            P("tp", "fsdp"),
-            P(None, "fsdp", "tp"),
-            P("tp", "fsdp"),
-            P("fsdp", "tp"),
-            P("tp", "fsdp"),
-        ),
-        out_specs=(
-            P("fsdp", "ctx", None),
-            P("fsdp", "ctx", None),
-            P(None, "fsdp"),
-            P(None, "fsdp"),
-            P("tp", "fsdp"),
-            P(None, "fsdp", "tp"),
-            P("tp", "fsdp"),
-            P("fsdp", "tp"),
-            P("tp", "fsdp"),
-            P("fsdp", "ctx", None),
-            P("fsdp", "ctx", None),
-            P(None, "fsdp"),
-            P(None, "fsdp"),
-            P("tp", "fsdp"),
-            P(None, "fsdp", "tp"),
-            P("tp", "fsdp"),
-            P("fsdp", "tp"),
-            P("tp", "fsdp"),
-        ),
-        check_vma=False,
-    )
+        body, mesh=mesh, in_specs=one + one, out_specs=grads + grads, check_vma=False
+    )

time: 1450 us -> 743 us (0.51)
  the two profiles are of different devices: /device:TPU:0 before, /device:TPU:8 now
where the time goes in v1:
time: 743 us; the launch traced here: 731 us
  waiting for transfers between devices  252 us (34%)
  local copies, waits for them, and re-layouts  155 us (21%)
  starting transfers between devices  114 us (15%)
  other arithmetic  76.7 us (10%)
  Pallas kernels  73.4 us (10%)
  matrix products  55.2 us (7%)
    ppermute x24, waiting for transfers between devices, swap_blocks(): lax.ppermute(pick(here ^ step), 'ctx', pairs)  113 us
    dot_general x24, matrix products, dot(): lax.dot_general(left, right, (dims, ((), ())), preferred_element_type=F32)  55.2 us
    ppermute x12, waiting for transfers between devices, reduce_owned(): lax.ppermute(total, 'ctx', pairs)[None]  40 us
    pallas_call x2, Pallas kernels, attend_back(): pl.pallas_call(kernel, grid_spec=pltpu.PrefetchScalarGridSpec(num_scalar_...  38.3 us
    pallas_call x2, Pallas kernels, attend(): pl.pallas_call(kernel, grid_spec=pltpu.PrefetchScalarGridSpec(num_scalar_...  35.1 us
    ppermute x4, waiting for transfers between devices, reduce_owned(): lax.ppermute(pair(group ^ 2, group ^ 3, half), 'fsdp', ACROSS_Y).astype(F32)  30.3 us
    ppermute x12, waiting for transfers between devices, reduce_owned(): lax.ppermute(cut(owned_low, here ^ step), 'ctx', pairs).astype(F32)  28.5 us
    ppermute x24, starting transfers between devices, swap_blocks(): lax.ppermute(pick(here ^ step), 'ctx', pairs)  26.1 us
  transfers between devices with their start and end apart: 92, of which 44 were waited for; matrix products, arithmetic and copies ran while one was open for 34% of the time, Pallas kernels for 7%

profile of v1, /device:TPU:8, one launch (start us, length us, event | category | flops | bytes accessed | tf_op | source)
XLA Modules:
  0.0 730.6 jit_solution(12818604539691462947)
XLA Ops:
  48.5 9.1 %collective-permute-done.26 = bf16[72,768]{0,1:T(8,128)(2,1)} collective-permute-done((bf16[72,768]{0,1:T(8,128)(2,1)}, bf16[72,768]{0,1:T(8,128)(2,1)}, u32[]{:S(2)}, u32[]{:S(2)}) %collective-permute-start.26) | collective-permute-done | bytes 110624 | tf_op jit(solution)/shard_map/ppermute | solution.py:31
  60.9 12.4 %collective-permute-done.27 = bf16[72,768]{0,1:T(8,128)(2,1)S(1)} collective-permute-done((bf16[72,768]{0,1:T(8,128)(2,1)}, bf16[72,768]{0,1:T(8,128)(2,1)S(1)}, u32[]{:S(2)}, u32[]{:S(2)}) %collective-permute-start.27) | collective-permute-done | bytes 110624 | tf_op jit(solution)/shard_map/ppermute | solution.py:32
  103.0 6.6 collective-permute-done.29
  110.2 4.2 collective-permute-done.30
  116.9 13.3 %attend_causal.1 = (bf16[2048,128]{1,0:T(8,128)(2,1)}, f32[8,16,256]{2,1,0:T(8,128)}) custom-call(s32[3,8]{1,0:T(4,128)} %get-tuple-element.370.bounds, bf16[2048,128]{1,0:T(8,128)(2,1)} %bitcast.517, bf16[2048,128]{1,0:T(8,128)(2,1)} %bitcast.515, s32[2048,1]{1,0:T(8,128)} %copy.330.rest_0_.sc, s32[1,2048]{1,0:T(1,128)} %sr.1), custom_call_target="tpu_custom_call" | custom-call | flops 2147483648 | bytes 1572864 | tf_op jit(solution)/shard_map/attend_causal/pallas_call | solution.py:198
  132.3 3.2 collective-permute-start.32
  139.5 4.2 fusion.214
  156.1 5.2 collective-permute-done.33
  167.8 7.5 %collective-permute-done.4 = bf16[1,3,512,128]{3,2,1,0:T(8,128)(2,1)S(1)} collective-permute-done((bf16[1,3,512,128]{3,2,1,0:T(8,128)(2,1)}, bf16[1,3,512,128]{3,2,1,0:T(8,128)(2,1)S(1)}, u32[]{:S(2)}, u32[]{:S(2)}) %collective-permute-start.4) | collective-permute-done | bytes 393248 | tf_op jit(solution)/shard_map/ppermute | solution.py:56
  175.4 14.1 %collective-permute-done.5 = bf16[1,3,512,128]{3,2,1,0:T(8,128)(2,1)S(1)} collective-permute-done((bf16[1,3,512,128]{3,2,1,0:T(8,128)(2,1)S(1)}, bf16[1,3,512,128]{3,2,1,0:T(8,128)(2,1)S(1)}, u32[]{:S(2)}, u32[]{:S(2)}) %collective-permute-start.5) | collective-permute-done | bytes 393248 | tf_op jit(solution)/shard_map/ppermute | solution.py:56
  189.6 6.4 collective-permute-done.6
  197.3 21.8 %attend_full.1 = (bf16[2048,128]{1,0:T(8,128)(2,1)}, f32[8,16,256]{2,1,0:T(8,128)}) custom-call(s32[3,8]{1,0:T(4,128)} %get-tuple-element.371.bounds, bf16[2048,128]{1,0:T(8,128)(2,1)} %bitcast.513, bf16[2048,128]{1,0:T(8,128)(2,1)} %bitcast.511, bf16[2048,128]{1,0:T(8,128)(2,1)} %bitcast.509, s32[2048,1]{1,0:T(8,128)} %copy.299.segcol_ref, s32[1,2048]{1,0:T(1,128)} %segrow_ref.3), custom_call_target="tpu_custom_call" | custom-call | flops 4294967296 | bytes 1572864 | tf_op jit(solution)/shard_map/attend_full/pallas_call | solution.py:198
  222.0 3.4 collective-permute-done.7
  226.5 6.9 collective-permute-done.9
  241.3 8.2 %collective-permute-start.13 = (bf16[96,3456]{1,0:T(8,128)(2,1)S(1)}, bf16[96,3456]{1,0:T(8,128)(2,1)S(1)}, u32[]{:S(2)}, u32[]{:S(2)}) collective-permute-start(bf16[96,3456]{1,0:T(8,128)(2,1)S(1)} %slice.906), channel_id=1, source_target_pairs={{0,16},{8,24},{16,0},{24,8},{1,17},{9,25},{17,1},{25,9},{2,18},{10... | collective-permute-start | bytes 1990664 | tf_op jit(solution)/shard_map/ppermute | solution.py:32
  258.7 3.1 convert_reduce_fusion.2
  286.8 3.7 collective-permute-done.41
  295.3 15.0 %attend_back_causal.1 = (bf16[2048,128]{1,0:T(8,128)(2,1)}, bf16[2048,128]{1,0:T(8,128)(2,1)}) custom-call(s32[3,8]{1,0:T(4,128)} %get-tuple-element.370.bounds, bf16[2048,128]{1,0:T(8,128)(2,1)} %bitcast.518, bf16[2048,128]{1,0:T(8,128)(2,1)} %bitcast.119.do, bf16[2048,128]{1,0:T(8,128)(2,1)} %get-tuple-element.32.o, f32[8,16,256]{2,1,0:T(8,128)} %get-tuple-element.33.lse, ...), custom_call_target="tpu_custom_call" | custom-call | flops 5368709120 | bytes 3145728 | tf_op jit(solution)/shard_map/attend_back_causal/pallas_call | solution.py:329
  320.1 3.7 collective-permute-done.43
  325.6 9.3 %collective-permute-done.44 = bf16[1,2,512,128]{3,2,0,1:T(8,128)(2,1)} collective-permute-done((bf16[1,2,512,128]{3,2,0,1:T(8,128)(2,1)}, bf16[1,2,512,128]{3,2,0,1:T(8,128)(2,1)}, u32[]{:S(2)}, u32[]{:S(2)}) %collective-permute-start.44) | collective-permute-done | bytes 262176 | tf_op jit(solution)/shard_map/ppermute | solution.py:56
  336.6 3.1 collective-permute-done.45
  346.5 3.4 concatenate.206
  359.6 3.2 convolution_add_fusion
  362.8 4.7 fusion.6
  367.5 4.3 convert_reduce_fusion
  375.0 4.2 fusion.8
  389.0 3.1 convolution_convert_fusion.1
  400.6 5.7 collective-permute-done.85
  414.6 5.8 collective-permute-done.88
  445.8 3.5 multiply_reduce_fusion
  449.3 3.8 fusion.182
  462.2 4.1 collective-permute-done.18
  470.2 23.3 %attend_back_full.1 = (bf16[2048,128]{1,0:T(8,128)(2,1)}, bf16[2048,128]{1,0:T(8,128)(2,1)}, bf16[2048,128]{1,0:T(8,128)(2,1)}) custom-call(s32[3,8]{1,0:T(4,128)} %get-tuple-element.371.bounds, bf16[2048,128]{1,0:T(8,128)(2,1)} %bitcast.514, bf16[2048,128]{1,0:T(8,128)(2,1)} %bitcast.506, bf16[2048,128]{1,0:T(8,128)(2,1)} %get-tuple-element.27.o_ref, ...), custom_call_target="tpu_custom_call" | custom-call | flops 10737418240 | bytes 3145728 | tf_op jit(solution)/shard_map/attend_back_full/pallas_call | solution.py:329
  502.0 7.2 collective-permute-done.20
  509.3 13.4 %collective-permute-done.21 = bf16[1,3,512,128]{3,2,0,1:T(8,128)(2,1)S(1)} collective-permute-done((bf16[1,3,512,128]{3,2,0,1:T(8,128)(2,1)S(1)}, bf16[1,3,512,128]{3,2,0,1:T(8,128)(2,1)S(1)}, u32[]{:S(2)}, u32[]{:S(2)}) %collective-permute-start.21) | collective-permute-done | bytes 393248 | tf_op jit(solution)/shard_map/ppermute | solution.py:56
  522.8 8.9 %collective-permute-done.22 = bf16[1,3,512,128]{3,2,0,1:T(8,128)(2,1)S(1)} collective-permute-done((bf16[1,3,512,128]{3,2,0,1:T(8,128)(2,1)S(1)}, bf16[1,3,512,128]{3,2,0,1:T(8,128)(2,1)S(1)}, u32[]{:S(2)}, u32[]{:S(2)}) %collective-permute-start.22) | collective-permute-done | bytes 393248 | tf_op jit(solution)/shard_map/ppermute | solution.py:56
  538.1 4.1 concatenate.187
  548.1 8.5 %collective-permute-start.63 = (bf16[192,3456]{1,0:T(8,128)(2,1)}, bf16[192,3456]{1,0:T(8,128)(2,1)}, u32[]{:S(2)}, u32[]{:S(2)}) collective-permute-start(bf16[192,3456]{1,0:T(8,128)(2,1)} %pad_maximum_fusion.8), channel_id=1, source_target_pairs={{0,16},{8,24},{16,0},{24,8},{1,17},{9,25},{17,1},{25,9},{2,18},{10... | collective-permute-start | bytes 3981320 | tf_op jit(solution)/shard_map/ppermute | solution.py:83
  556.8 7.5 %collective-permute-start.52 = (bf16[96,1152]{1,0:T(8,128)(2,1)S(1)}, bf16[96,1152]{1,0:T(8,128)(2,1)S(1)}, u32[]{:S(2)}, u32[]{:S(2)}) collective-permute-start(bf16[96,1152]{1,0:T(8,128)(2,1)S(1)} %fusion.117), channel_id=1, source_target_pairs={{0,16},{8,24},{16,0},{24,8},{1,17},{9,25},{17,1},{25,9},{2,18},{10... | collective-permute-start | bytes 663560 | tf_op jit(solution)/shard_map/ppermute | solution.py:86
  566.0 30.3 %collective-permute-done.53 = bf16[192,1152]{1,0:T(8,128)(2,1)S(1)} collective-permute-done((bf16[192,1152]{1,0:T(8,128)(2,1)S(1)}, bf16[192,1152]{1,0:T(8,128)(2,1)S(1)}, u32[]{:S(2)}, u32[]{:S(2)}) %collective-permute-start.53) | collective-permute-done | bytes 442400 | tf_op jit(solution)/shard_map/ppermute | solution.py:83
  623.9 3.0 convert_element_type.534
  630.4 4.7 collective-permute-done.59
  648.8 3.8 collective-permute-done.48
  671.5 16.2 %collective-permute-done.67 = bf16[48,3456]{1,0:T(8,128)(2,1)} collective-permute-done((bf16[48,3456]{1,0:T(8,128)(2,1)}, bf16[48,3456]{1,0:T(8,128)(2,1)}, u32[]{:S(2)}, u32[]{:S(2)}) %collective-permute-start.67) | collective-permute-done | bytes 331808 | tf_op jit(solution)/shard_map/ppermute | solution.py:100
  687.7 4.0 collective-permute-done.66
  699.2 7.0 collective-permute-done.68
  706.2 14.6 %collective-permute-done.69 = bf16[48,3456]{1,0:T(8,128)(2,1)S(1)} collective-permute-done((bf16[48,3456]{1,0:T(8,128)(2,1)S(1)}, bf16[48,3456]{1,0:T(8,128)(2,1)S(1)}, u32[]{:S(2)}, u32[]{:S(2)}) %collective-permute-start.69) | collective-permute-done | bytes 331808 | tf_op jit(solution)/shard_map/ppermute | solution.py:107
  720.9 6.6 collective-permute-done.70
  (773 shorter events, 353.7 us)
Async XLA Ops:
  3.6 83.7 %collective-permute-start = (bf16[208,1152]{1,0:T(8,128)(2,1)}, bf16[208,1152]{1,0:T(8,128)(2,1)}, u32[]{:S(2)}, u32[]{:S(2)}) collective-permute-start(bf16[208,1152]{1,0:T(8,128)(2,1)} %constant_dynamic-update-slice_fusion.40), channel_id=1, source_target_pairs={{0,8},{8,0},{16,24},{24,16},{1,9},{9,1},{17,25},{25,17},{2,10},{10... | collective-permute-start | bytes 1437704 | tf_op jit(solution)/shard_map/ppermute | solution.py:29
  5.0 78.2 %collective-permute-start.1 = (bf16[208,1152]{1,0:T(8,128)(2,1)}, bf16[208,1152]{1,0:T(8,128)(2,1)}, u32[]{:S(2)}, u32[]{:S(2)}) collective-permute-start(bf16[208,1152]{1,0:T(8,128)(2,1)} %constant_dynamic-update-slice_fusion.40), channel_id=1, source_target_pairs={{0,16},{8,24},{16,0},{24,8},{1,17},{9,25},{17,1},{25,9},{2,18},{10... | collective-permute-start | bytes 1437704 | tf_op jit(solution)/shard_map/ppermute | solution.py:30
  7.8 34.7 %collective-permute-start.24 = (bf16[144,768]{0,1:T(8,128)(2,1)}, bf16[144,768]{0,1:T(8,128)(2,1)}, u32[]{:S(2)}, u32[]{:S(2)}) collective-permute-start(bf16[144,768]{0,1:T(8,128)(2,1)} %pad_maximum_fusion.23), channel_id=1, source_target_pairs={{0,8},{8,0},{16,24},{24,16},{1,9},{9,1},{17,25},{25,17},{2,10},{10... | collective-permute-start | bytes 663560 | tf_op jit(solution)/shard_map/ppermute | solution.py:29
  8.4 30.9 %collective-permute-start.25 = (bf16[144,768]{0,1:T(8,128)(2,1)}, bf16[144,768]{0,1:T(8,128)(2,1)}, u32[]{:S(2)}, u32[]{:S(2)}) collective-permute-start(bf16[144,768]{0,1:T(8,128)(2,1)} %pad_maximum_fusion.23), channel_id=1, source_target_pairs={{0,16},{8,24},{16,0},{24,8},{1,17},{9,25},{17,1},{25,9},{2,18},{10... | collective-permute-start | bytes 663560 | tf_op jit(solution)/shard_map/ppermute | solution.py:30
  13.3 226.8 %collective-permute-start.10 = (bf16[192,3456]{1,0:T(8,128)(2,1)}, bf16[192,3456]{1,0:T(8,128)(2,1)}, u32[]{:S(2)}, u32[]{:S(2)}) collective-permute-start(bf16[192,3456]{1,0:T(8,128)(2,1)} %get-tuple-element.216), channel_id=1, source_target_pairs={{0,8},{8,0},{16,24},{24,16},{1,9},{9,1},{17,25},{25,17},{2,10},{10... | collective-permute-start | bytes 3981320 | tf_op jit(solution)/shard_map/ppermute | solution.py:29
  39.3 199.6 %collective-permute-start.11 = (bf16[192,3456]{1,0:T(8,128)(2,1)}, bf16[192,3456]{1,0:T(8,128)(2,1)}, u32[]{:S(2)}, u32[]{:S(2)}) collective-permute-start(bf16[192,3456]{1,0:T(8,128)(2,1)} %get-tuple-element.216), channel_id=1, source_target_pairs={{0,16},{8,24},{16,0},{24,8},{1,17},{9,25},{17,1},{25,9},{2,18},{10... | collective-permute-start | bytes 3981320 | tf_op jit(solution)/shard_map/ppermute | solution.py:30
  42.5 15.1 %collective-permute-start.26 = (bf16[72,768]{0,1:T(8,128)(2,1)}, bf16[72,768]{0,1:T(8,128)(2,1)}, u32[]{:S(2)}, u32[]{:S(2)}) collective-permute-start(bf16[72,768]{0,1:T(8,128)(2,1)} %slice.955), channel_id=1, source_target_pairs={{0,8},{8,0},{16,24},{24,16},{1,9},{9,1},{17,25},{25,17},{2,10},{10... | collective-permute-start | bytes 331784 | tf_op jit(solution)/shard_map/ppermute | solution.py:31
  57.6 15.6 %collective-permute-start.27 = (bf16[72,768]{0,1:T(8,128)(2,1)}, bf16[72,768]{0,1:T(8,128)(2,1)S(1)}, u32[]{:S(2)}, u32[]{:S(2)}) collective-permute-start(bf16[72,768]{0,1:T(8,128)(2,1)} %slice.956), channel_id=1, source_target_pairs={{0,16},{8,24},{16,0},{24,8},{1,17},{9,25},{17,1},{25,9},{2,18},{10... | collective-permute-start | bytes 331784 | tf_op jit(solution)/shard_map/ppermute | solution.py:32
  73.3 18.2 %collective-permute-start.34 = (bf16[128,2304]{1,0:T(8,128)(2,1)}, bf16[128,2304]{1,0:T(8,128)(2,1)}, u32[]{:S(2)}, u32[]{:S(2)}) collective-permute-start(bf16[128,2304]{1,0:T(8,128)(2,1)} %get-tuple-element.258), channel_id=1, source_target_pairs={{0,8},{8,0},{16,24},{24,16},{1,9},{9,1},{17,25},{25,17},{2,10},{10... | collective-permute-start | bytes 1769480 | tf_op jit(solution)/shard_map/ppermute | solution.py:29
  87.2 14.3 %collective-permute-start.28 = (bf16[1,2,512,128]{3,2,1,0:T(8,128)(2,1)S(1)}, bf16[1,2,512,128]{3,2,1,0:T(8,128)(2,1)S(1)}, u32[]{:S(2)}, u32[]{:S(2)}) collective-permute-start(bf16[1,2,512,128]{3,2,1,0:T(8,128)(2,1)S(1)} %get-tuple-element.243), channel_id=1, source_target_pairs={{0,2},{2,0},{4,6},{6,4},{1,3},{3,1},{5,7},{7,5},{8,10},{10,8},{12,... | collective-permute-start | bytes 786440 | tf_op jit(solution)/shard_map/ppermute | solution.py:56
  91.5 18.1 %collective-permute-start.29 = (bf16[1,2,512,128]{3,2,1,0:T(8,128)(2,1)S(1)}, bf16[1,2,512,128]{3,2,1,0:T(8,128)(2,1)S(1)}, u32[]{:S(2)}, u32[]{:S(2)}) collective-permute-start(bf16[1,2,512,128]{3,2,1,0:T(8,128)(2,1)S(1)} %get-tuple-element.242), channel_id=1, source_target_pairs={{0,4},{2,6},{4,0},{6,2},{1,5},{3,7},{5,1},{7,3},{8,12},{10,14},{12... | collective-permute-start | bytes 786440 | tf_op jit(solution)/shard_map/ppermute | solution.py:56
  96.6 17.7 %collective-permute-start.30 = (bf16[1,2,512,128]{3,2,1,0:T(8,128)(2,1)S(1)}, bf16[1,2,512,128]{3,2,1,0:T(8,128)(2,1)S(1)}, u32[]{:S(2)}, u32[]{:S(2)}) collective-permute-start(bf16[1,2,512,128]{3,2,1,0:T(8,128)(2,1)S(1)} %get-tuple-element.241), channel_id=1, source_target_pairs={{0,6},{2,4},{4,2},{6,0},{1,7},{3,5},{5,3},{7,1},{8,14},{10,12},{12... | collective-permute-start | bytes 786440 | tf_op jit(solution)/shard_map/ppermute | solution.py:56
  101.6 30.6 %collective-permute-start.2 = (bf16[104,1152]{1,0:T(8,128)(2,1)}, bf16[104,1152]{1,0:T(8,128)(2,1)S(1)}, u32[]{:S(2)}, u32[]{:S(2)}) collective-permute-start(bf16[104,1152]{1,0:T(8,128)(2,1)} %slice.859), channel_id=1, source_target_pairs={{0,8},{8,0},{16,24},{24,16},{1,9},{9,1},{17,25},{25,17},{2,10},{10... | collective-permute-start | bytes 718856 | tf_op jit(solution)/shard_map/ppermute | solution.py:31
  109.6 22.7 %collective-permute-start.3 = (bf16[104,1152]{1,0:T(8,128)(2,1)}, bf16[104,1152]{1,0:T(8,128)(2,1)}, u32[]{:S(2)}, u32[]{:S(2)}) collective-permute-start(bf16[104,1152]{1,0:T(8,128)(2,1)} %slice.860), channel_id=1, source_target_pairs={{0,16},{8,24},{16,0},{24,8},{1,17},{9,25},{17,1},{25,9},{2,18},{10... | collective-permute-start | bytes 718856 | tf_op jit(solution)/shard_map/ppermute | solution.py:32
  114.3 48.0 %collective-permute-start.36 = (bf16[64,2304]{1,0:T(8,128)(2,1)}, bf16[64,2304]{1,0:T(8,128)(2,1)}, u32[]{:S(2)}, u32[]{:S(2)}) collective-permute-start(bf16[64,2304]{1,0:T(8,128)(2,1)} %slice.990), channel_id=1, source_target_pairs={{0,8},{8,0},{16,24},{24,16},{1,9},{9,1},{17,25},{25,17},{2,10},{10... | collective-permute-start | bytes 884744 | tf_op jit(solution)/shard_map/ppermute | solution.py:31
  132.1 22.6 %collective-permute-start.31 = (bf16[1,512,128]{2,1,0:T(8,128)(2,1)}, bf16[1,512,128]{2,1,0:T(8,128)(2,1)}, u32[]{:S(2)}, u32[]{:S(2)}) collective-permute-start(bf16[1,512,128]{2,1,0:T(8,128)(2,1)} %get-tuple-element.271), channel_id=1, source_target_pairs={{0,2},{2,0},{4,6},{6,4},{1,3},{3,1},{5,7},{7,5},{8,10},{10,8},{12,... | collective-permute-start | bytes 393224 | tf_op jit(solution)/shard_map/ppermute | solution.py:56
  132.3 23.7 %collective-permute-start.32 = (bf16[1,512,128]{2,1,0:T(8,128)(2,1)}, bf16[1,512,128]{2,1,0:T(8,128)(2,1)S(1)}, u32[]{:S(2)}, u32[]{:S(2)}) collective-permute-start(bf16[1,512,128]{2,1,0:T(8,128)(2,1)} %get-tuple-element.270), channel_id=1, source_target_pairs={{0,4},{2,6},{4,0},{6,2},{1,5},{3,7},{5,1},{7,3},{8,12},{10,14},{12... | collective-permute-start | bytes 393224 | tf_op jit(solution)/shard_map/ppermute | solution.py:56
  161.3 14.1 %collective-permute-start.4 = (bf16[1,3,512,128]{3,2,1,0:T(8,128)(2,1)}, bf16[1,3,512,128]{3,2,1,0:T(8,128)(2,1)S(1)}, u32[]{:S(2)}, u32[]{:S(2)}) collective-permute-start(bf16[1,3,512,128]{3,2,1,0:T(8,128)(2,1)} %get-tuple-element.212), channel_id=1, source_target_pairs={{0,2},{2,0},{4,6},{6,4},{1,3},{3,1},{5,7},{7,5},{8,10},{10,8},{12,... | collective-permute-start | bytes 1179656 | tf_op jit(solution)/shard_map/ppermute | solution.py:56
  162.4 27.2 %collective-permute-start.5 = (bf16[1,3,512,128]{3,2,1,0:T(8,128)(2,1)S(1)}, bf16[1,3,512,128]{3,2,1,0:T(8,128)(2,1)S(1)}, u32[]{:S(2)}, u32[]{:S(2)}) collective-permute-start(bf16[1,3,512,128]{3,2,1,0:T(8,128)(2,1)S(1)} %copy-done.52), channel_id=1, source_target_pairs={{0,4},{2,6},{4,0},{6,2},{1,5},{3,7},{5,1},{7,3},{8,12},{10,14},{12... | collective-permute-start | bytes 1179656 | tf_op jit(solution)/shard_map/ppermute | solution.py:56
  165.4 30.6 %collective-permute-start.6 = (bf16[1,3,512,128]{3,2,1,0:T(8,128)(2,1)S(1)}, bf16[1,3,512,128]{3,2,1,0:T(8,128)(2,1)S(1)}, u32[]{:S(2)}, u32[]{:S(2)}) collective-permute-start(bf16[1,3,512,128]{3,2,1,0:T(8,128)(2,1)S(1)} %copy-done.51), channel_id=1, source_target_pairs={{0,6},{2,4},{4,2},{6,0},{1,7},{3,5},{5,3},{7,1},{8,14},{10,12},{12... | collective-permute-start | bytes 1179656 | tf_op jit(solution)/shard_map/ppermute | solution.py:56
  221.9 32.6 %collective-permute-start.38 = (f32[512,512]{0,1:T(8,128)S(1)}, f32[512,512]{0,1:T(8,128)}, u32[]{:S(2)}, u32[]{:S(2)}) collective-permute-start(f32[512,512]{0,1:T(8,128)S(1)} %fusion.141), channel_id=1, source_target_pairs={{0,1},{1,0},{2,3},{3,2},{4,5},{5,4},{6,7},{7,6},{8,9},{9,8},{10,11... | collective-permute-start | bytes 3145736 | tf_op jit(solution)/shard_map/ppermute | solution.py:62
  240.1 27.9 %collective-permute-start.12 = (bf16[96,3456]{1,0:T(8,128)(2,1)S(1)}, bf16[96,3456]{1,0:T(8,128)(2,1)S(1)}, u32[]{:S(2)}, u32[]{:S(2)}) collective-permute-start(bf16[96,3456]{1,0:T(8,128)(2,1)S(1)} %slice.905), channel_id=1, source_target_pairs={{0,8},{8,0},{16,24},{24,16},{1,9},{9,1},{17,25},{25,17},{2,10},{10... | collective-permute-start | bytes 1990664 | tf_op jit(solution)/shard_map/ppermute | solution.py:31
  241.3 27.5 %collective-permute-start.13 = (bf16[96,3456]{1,0:T(8,128)(2,1)S(1)}, bf16[96,3456]{1,0:T(8,128)(2,1)S(1)}, u32[]{:S(2)}, u32[]{:S(2)}) collective-permute-start(bf16[96,3456]{1,0:T(8,128)(2,1)S(1)} %slice.906), channel_id=1, source_target_pairs={{0,16},{8,24},{16,0},{24,8},{1,17},{9,25},{17,1},{25,9},{2,18},{10... | collective-permute-start | bytes 1990664 | tf_op jit(solution)/shard_map/ppermute | solution.py:32
  271.4 85.7 %collective-permute-start.14 = (f32[512,768]{1,0:T(8,128)S(1)}, f32[512,768]{1,0:T(8,128)}, u32[]{:S(2)}, u32[]{:S(2)}) collective-permute-start(f32[512,768]{1,0:T(8,128)S(1)} %fusion.113), channel_id=1, source_target_pairs={{0,1},{1,0},{2,3},{3,2},{4,5},{5,4},{6,7},{7,6},{8,9},{9,8},{10,11... | collective-permute-start | bytes 4718600 | tf_op jit(solution)/shard_map/ppermute | solution.py:62
  314.9 20.0 %collective-permute-start.44 = (bf16[1,2,512,128]{3,2,0,1:T(8,128)(2,1)}, bf16[1,2,512,128]{3,2,0,1:T(8,128)(2,1)}, u32[]{:S(2)}, u32[]{:S(2)}) collective-permute-start(bf16[1,2,512,128]{3,2,0,1:T(8,128)(2,1)} %get-tuple-element.238), channel_id=1, source_target_pairs={{0,4},{2,6},{4,0},{6,2},{1,5},{3,7},{5,1},{7,3},{8,12},{10,14},{12... | collective-permute-start | bytes 786440 | tf_op jit(solution)/shard_map/ppermute | solution.py:56
  316.6 23.1 %collective-permute-start.45 = (bf16[1,2,512,128]{3,2,0,1:T(8,128)(2,1)S(1)}, bf16[1,2,512,128]{3,2,0,1:T(8,128)(2,1)}, u32[]{:S(2)}, u32[]{:S(2)}) collective-permute-start(bf16[1,2,512,128]{3,2,0,1:T(8,128)(2,1)S(1)} %get-tuple-element.235), channel_id=1, source_target_pairs={{0,6},{2,4},{4,2},{6,0},{1,7},{3,5},{5,3},{7,1},{8,14},{10,12},{12... | collective-permute-start | bytes 786440 | tf_op jit(solution)/shard_map/ppermute | solution.py:56
  320.1 72.0 %collective-permute-start.84 = (bf16[128,2304]{1,0:T(8,128)(2,1)}, bf16[128,2304]{1,0:T(8,128)(2,1)}, u32[]{:S(2)}, u32[]{:S(2)}) collective-permute-start(bf16[128,2304]{1,0:T(8,128)(2,1)} %pad_maximum_fusion.13), channel_id=1, source_target_pairs={{0,16},{8,24},{16,0},{24,8},{1,17},{9,25},{17,1},{25,9},{2,18},{10... | collective-permute-start | bytes 1769480 | tf_op jit(solution)/shard_map/ppermute | solution.py:83
  323.9 55.4 %collective-permute-start.82 = (bf16[128,2304]{1,0:T(8,128)(2,1)}, bf16[128,2304]{1,0:T(8,128)(2,1)}, u32[]{:S(2)}, u32[]{:S(2)}) collective-permute-start(bf16[128,2304]{1,0:T(8,128)(2,1)} %pad_maximum_fusion.12), channel_id=1, source_target_pairs={{0,8},{8,0},{16,24},{24,16},{1,9},{9,1},{17,25},{25,17},{2,10},{10... | collective-permute-start | bytes 1769480 | tf_op jit(solution)/shard_map/ppermute | solution.py:82
  351.9 28.6 %collective-permute-start.74 = (bf16[128,768]{1,0:T(8,128)(2,1)S(1)}, bf16[128,768]{1,0:T(8,128)(2,1)S(1)}, u32[]{:S(2)}, u32[]{:S(2)}) collective-permute-start(bf16[128,768]{1,0:T(8,128)(2,1)S(1)} %pad_maximum_fusion.26), channel_id=1, source_target_pairs={{0,16},{8,24},{16,0},{24,8},{1,17},{9,25},{17,1},{25,9},{2,18},{10... | collective-permute-start | bytes 589832 | tf_op jit(solution)/shard_map/ppermute | solution.py:83
  352.0 22.7 %collective-permute-start.72 = (bf16[128,768]{1,0:T(8,128)(2,1)S(1)}, bf16[128,768]{1,0:T(8,128)(2,1)S(1)}, u32[]{:S(2)}, u32[]{:S(2)}) collective-permute-start(bf16[128,768]{1,0:T(8,128)(2,1)S(1)} %pad_maximum_fusion.25), channel_id=1, source_target_pairs={{0,8},{8,0},{16,24},{24,16},{1,9},{9,1},{17,25},{25,17},{2,10},{10... | collective-permute-start | bytes 589832 | tf_op jit(solution)/shard_map/ppermute | solution.py:82
  392.1 35.0 %collective-permute-start.46 = (f32[512,512]{0,1:T(8,128)}, f32[512,512]{0,1:T(8,128)}, u32[]{:S(2)}, u32[]{:S(2)}) collective-permute-start(f32[512,512]{0,1:T(8,128)} %fusion.217), channel_id=1, source_target_pairs={{0,1},{1,0},{2,3},{3,2},{4,5},{5,4},{6,7},{7,6},{8,9},{9,8},{10,11... | collective-permute-start | bytes 3145736 | tf_op jit(solution)/shard_map/ppermute | solution.py:62
  393.3 52.5 %collective-permute-start.16 = (f32[512,768]{1,0:T(8,128)}, f32[512,768]{1,0:T(8,128)}, u32[]{:S(2)}, u32[]{:S(2)}) collective-permute-start(f32[512,768]{1,0:T(8,128)} %fusion.8), channel_id=1, source_target_pairs={{0,1},{1,0},{2,3},{3,2},{4,5},{5,4},{6,7},{7,6},{8,9},{9,8},{10,11... | collective-permute-start | bytes 4718600 | tf_op jit(solution)/shard_map/ppermute | solution.py:62
  396.8 14.9 %collective-permute-start.81 = (bf16[32,768]{1,0:T(8,128)(2,1)S(1)}, bf16[32,768]{1,0:T(8,128)(2,1)S(1)}, u32[]{:S(2)}, u32[]{:S(2)}) collective-permute-start(bf16[32,768]{1,0:T(8,128)(2,1)S(1)} %get-tuple-element.155), channel_id=1, source_target_pairs={{0,6},{2,4},{4,2},{6,0},{1,7},{3,5},{5,3},{7,1},{8,14},{10,12},{12... | collective-permute-start | bytes 147464 | tf_op jit(solution)/shard_map/ppermute | solution.py:107
  420.5 28.8 %collective-permute-start.15 = (f32[512,768]{1,0:T(8,128)}, f32[512,768]{1,0:T(8,128)}, u32[]{:S(2)}, u32[]{:S(2)}) collective-permute-start(f32[512,768]{1,0:T(8,128)} %fusion.6), channel_id=1, source_target_pairs={{0,1},{1,0},{2,3},{3,2},{4,5},{5,4},{6,7},{7,6},{8,9},{9,8},{10,11... | collective-permute-start | bytes 4718600 | tf_op jit(solution)/shard_map/ppermute | solution.py:62
  495.6 27.2 %collective-permute-start.21 = (bf16[1,3,512,128]{3,2,0,1:T(8,128)(2,1)S(1)}, bf16[1,3,512,128]{3,2,0,1:T(8,128)(2,1)S(1)}, u32[]{:S(2)}, u32[]{:S(2)}) collective-permute-start(bf16[1,3,512,128]{3,2,0,1:T(8,128)(2,1)S(1)} %get-tuple-element.203), channel_id=1, source_target_pairs={{0,4},{2,6},{4,0},{6,2},{1,5},{3,7},{5,1},{7,3},{8,12},{10,14},{12... | collective-permute-start | bytes 1179656 | tf_op jit(solution)/shard_map/ppermute | solution.py:56
  496.3 35.4 %collective-permute-start.22 = (bf16[1,3,512,128]{3,2,0,1:T(8,128)(2,1)S(1)}, bf16[1,3,512,128]{3,2,0,1:T(8,128)(2,1)S(1)}, u32[]{:S(2)}, u32[]{:S(2)}) collective-permute-start(bf16[1,3,512,128]{3,2,0,1:T(8,128)(2,1)S(1)} %get-tuple-element.202), channel_id=1, source_target_pairs={{0,6},{2,4},{4,2},{6,0},{1,7},{3,5},{5,3},{7,1},{8,14},{10,12},{12... | collective-permute-start | bytes 1179656 | tf_op jit(solution)/shard_map/ppermute | solution.py:56
  548.1 75.8 %collective-permute-start.63 = (bf16[192,3456]{1,0:T(8,128)(2,1)}, bf16[192,3456]{1,0:T(8,128)(2,1)}, u32[]{:S(2)}, u32[]{:S(2)}) collective-permute-start(bf16[192,3456]{1,0:T(8,128)(2,1)} %pad_maximum_fusion.8), channel_id=1, source_target_pairs={{0,16},{8,24},{16,0},{24,8},{1,17},{9,25},{17,1},{25,9},{2,18},{10... | collective-permute-start | bytes 3981320 | tf_op jit(solution)/shard_map/ppermute | solution.py:83
  556.6 39.7 %collective-permute-start.53 = (bf16[192,1152]{1,0:T(8,128)(2,1)S(1)}, bf16[192,1152]{1,0:T(8,128)(2,1)S(1)}, u32[]{:S(2)}, u32[]{:S(2)}) collective-permute-start(bf16[192,1152]{1,0:T(8,128)(2,1)S(1)} %pad_maximum_fusion.22), channel_id=1, source_target_pairs={{0,16},{8,24},{16,0},{24,8},{1,17},{9,25},{17,1},{25,9},{2,18},{10... | collective-permute-start | bytes 1327112 | tf_op jit(solution)/shard_map/ppermute | solution.py:83
  556.8 41.9 %collective-permute-start.52 = (bf16[96,1152]{1,0:T(8,128)(2,1)S(1)}, bf16[96,1152]{1,0:T(8,128)(2,1)S(1)}, u32[]{:S(2)}, u32[]{:S(2)}) collective-permute-start(bf16[96,1152]{1,0:T(8,128)(2,1)S(1)} %fusion.117), channel_id=1, source_target_pairs={{0,16},{8,24},{16,0},{24,8},{1,17},{9,25},{17,1},{25,9},{2,18},{10... | collective-permute-start | bytes 663560 | tf_op jit(solution)/shard_map/ppermute | solution.py:86
  565.5 48.7 %collective-permute-start.61 = (bf16[192,3456]{1,0:T(8,128)(2,1)}, bf16[192,3456]{1,0:T(8,128)(2,1)}, u32[]{:S(2)}, u32[]{:S(2)}) collective-permute-start(bf16[192,3456]{1,0:T(8,128)(2,1)} %pad_maximum_fusion.7), channel_id=1, source_target_pairs={{0,8},{8,0},{16,24},{24,16},{1,9},{9,1},{17,25},{25,17},{2,10},{10... | collective-permute-start | bytes 3981320 | tf_op jit(solution)/shard_map/ppermute | solution.py:82
  614.2 26.8 %collective-permute-start.23 = (f32[512,768]{1,0:T(8,128)}, f32[512,768]{1,0:T(8,128)}, u32[]{:S(2)}, u32[]{:S(2)}) collective-permute-start(f32[512,768]{1,0:T(8,128)} %fusion.216), channel_id=1, source_target_pairs={{0,1},{1,0},{2,3},{3,2},{4,5},{5,4},{6,7},{7,6},{8,9},{9,8},{10,11... | collective-permute-start | bytes 4718600 | tf_op jit(solution)/shard_map/ppermute | solution.py:62
  622.3 23.6 %collective-permute-start.62 = (bf16[96,3456]{1,0:T(8,128)(2,1)}, bf16[96,3456]{1,0:T(8,128)(2,1)}, u32[]{:S(2)}, u32[]{:S(2)}) collective-permute-start(bf16[96,3456]{1,0:T(8,128)(2,1)} %fusion.36), channel_id=1, source_target_pairs={{0,16},{8,24},{16,0},{24,8},{1,17},{9,25},{17,1},{25,9},{2,18},{10... | collective-permute-start | bytes 1990664 | tf_op jit(solution)/shard_map/ppermute | solution.py:86
  647.8 15.6 %collective-permute-start.64 = (bf16[96,3456]{1,0:T(8,128)(2,1)S(1)}, bf16[96,3456]{1,0:T(8,128)(2,1)S(1)}, u32[]{:S(2)}, u32[]{:S(2)}) collective-permute-start(bf16[96,3456]{1,0:T(8,128)(2,1)S(1)} %get-tuple-element.173), channel_id=1, source_target_pairs={{0,8},{8,0},{16,24},{24,16},{1,9},{9,1},{17,25},{25,17},{2,10},{10... | collective-permute-start | bytes 1990664 | tf_op jit(solution)/shard_map/ppermute | solution.py:87
  665.7 22.0 %collective-permute-start.67 = (bf16[48,3456]{1,0:T(8,128)(2,1)}, bf16[48,3456]{1,0:T(8,128)(2,1)}, u32[]{:S(2)}, u32[]{:S(2)}) collective-permute-start(bf16[48,3456]{1,0:T(8,128)(2,1)} %get-tuple-element.214), channel_id=1, source_target_pairs={{0,6},{2,4},{4,2},{6,0},{1,7},{3,5},{5,3},{7,1},{8,14},{10,12},{12... | collective-permute-start | bytes 995336 | tf_op jit(solution)/shard_map/ppermute | solution.py:100
  668.1 23.6 %collective-permute-start.66 = (bf16[48,3456]{1,0:T(8,128)(2,1)S(1)}, bf16[48,3456]{1,0:T(8,128)(2,1)}, u32[]{:S(2)}, u32[]{:S(2)}) collective-permute-start(bf16[48,3456]{1,0:T(8,128)(2,1)S(1)} %get-tuple-element.215), channel_id=1, source_target_pairs={{0,4},{2,6},{4,0},{6,2},{1,5},{3,7},{5,1},{7,3},{8,12},{10,14},{12... | collective-permute-start | bytes 995336 | tf_op jit(solution)/shard_map/ppermute | solution.py:100
  668.6 23.1 %collective-permute-start.65 = (bf16[48,3456]{1,0:T(8,128)(2,1)S(1)}, bf16[48,3456]{1,0:T(8,128)(2,1)}, u32[]{:S(2)}, u32[]{:S(2)}) collective-permute-start(bf16[48,3456]{1,0:T(8,128)(2,1)S(1)} %get-tuple-element.213), channel_id=1, source_target_pairs={{0,2},{2,0},{4,6},{6,4},{1,3},{3,1},{5,7},{7,5},{8,10},{10,8},{12,... | collective-permute-start | bytes 995336 | tf_op jit(solution)/shard_map/ppermute | solution.py:100
  697.6 23.2 %collective-permute-start.69 = (bf16[48,3456]{1,0:T(8,128)(2,1)S(1)}, bf16[48,3456]{1,0:T(8,128)(2,1)S(1)}, u32[]{:S(2)}, u32[]{:S(2)}) collective-permute-start(bf16[48,3456]{1,0:T(8,128)(2,1)S(1)} %get-tuple-element.157), channel_id=1, source_target_pairs={{0,4},{2,6},{4,0},{6,2},{1,5},{3,7},{5,1},{7,3},{8,12},{10,14},{12... | collective-permute-start | bytes 995336 | tf_op jit(solution)/shard_map/ppermute | solution.py:107
  698.6 28.9 %collective-permute-start.70 = (bf16[48,3456]{1,0:T(8,128)(2,1)S(1)}, bf16[48,3456]{1,0:T(8,128)(2,1)S(1)}, u32[]{:S(2)}, u32[]{:S(2)}) collective-permute-start(bf16[48,3456]{1,0:T(8,128)(2,1)S(1)} %get-tuple-element.157), channel_id=1, source_target_pairs={{0,6},{2,4},{4,2},{6,0},{1,7},{3,5},{5,3},{7,1},{8,14},{10,12},{12... | collective-permute-start | bytes 995336 | tf_op jit(solution)/shard_map/ppermute | solution.py:107
  (155 other events, 1269.9 us)

commit v2 on v0

v2 whole, which is shorter than its diff:
```python
import functools

import jax
import jax.numpy as jnp
from jax import lax
from jax.experimental import pallas as pl
from jax.experimental.pallas import tpu as pltpu
from jax.sharding import PartitionSpec as P

HD = 64
LANES = 128
QB = 256
KB = 512
NEG = -1e30
F32 = jnp.float32
MESH = pl.DeviceIdType.MESH
FSDP, CTX, TP = "fsdp", "ctx", "tp"
BF16 = jnp.bfloat16


def dot(left, right, dims=((1,), (0,))):
    return lax.dot_general(left, right, (dims, ((), ())), preferred_element_type=F32)


def reduce_small(vector):
    for axis, step in ((FSDP, 1), (FSDP, 2), (CTX, 1), (CTX, 2)):
        vector = vector + lax.ppermute(vector, axis, [(i, i ^ step) for i in range(4)])
    return vector


def lane_marks():
    lane = lax.broadcasted_iota(jnp.int32, (1, LANES), 1)
    first = (lane < HD).astype(F32).astype(BF16)
    second = (lane >= HD).astype(F32).astype(BF16)
    return first, second


def turn(value, flag):
    return jnp.where(flag != 0, pltpu.roll(value, HD, 1), value)


def attend_kernel(causal, bounds, m_ref, segcol_ref, segrow_ref, o_ref, lse_ref):
    block = pl.program_id(0)
    low, high, active = bounds[0, block], bounds[1, block], bounds[2, block]
    source, half = block // 2, block % 2
    first, second = lane_marks()
    lane = lax.broadcasted_iota(jnp.int32, (QB, LANES), 1)
    seg_query = segcol_ref[...]

    def one(query, load, own, other):
        def step(index, carry):
            top, acc = carry
            keys = load(index)
            scores = dot(query * own, keys, ((1,), (1,)))
            start = index * KB
            ok = seg_query == segrow_ref[:, pl.ds(pl.multiple_of(start, KB), KB)]
            if causal:
                key_pos = start + lax.broadcasted_iota(jnp.int32, (QB, KB), 1)
                query_pos = block * QB + lax.broadcasted_iota(jnp.int32, (QB, KB), 0)
                ok = jnp.logical_and(ok, key_pos <= query_pos)
            scores = jnp.where(ok, scores, NEG)
            new_top = jnp.maximum(top, jnp.max(scores, axis=1, keepdims=True))
            weights = jnp.exp(scores - new_top).astype(BF16)
            acc = acc * jnp.exp(top - new_top) + dot(weights, keys * other + own)
            return new_top, acc

        top, acc = lax.fori_loop(
            low, high, step, (jnp.full((QB, 1), NEG, F32), jnp.zeros((QB, LANES), F32))
        )
        return acc / pltpu.roll(acc, HD, 1), top + jnp.log(acc)

    if causal:
        query = turn(m_ref[source, :QB].astype(F32), half).astype(BF16)
        mixed, lse = one(query, lambda i: m_ref[i, QB:], first, second)
        mixed = turn(mixed, 1 - half).astype(BF16)
        lse_ref[0] = jnp.transpose(lse)[:16]

        @pl.when(half == 0)
        def _():
            o_ref[0] = mixed

        @pl.when(half != 0)
        def _():
            o_ref[0] = jnp.where(lane < HD, o_ref[0], mixed)
    else:
        query = m_ref[source, 0, pl.ds(pl.multiple_of(half * QB, QB), QB)]
        mixed, lse = one(query, lambda i: m_ref[i, 1], first, second)

        @pl.when(active == 0)
        def _():
            o_ref[0] = mixed.astype(BF16)
            lse_ref[0, :8] = jnp.transpose(lse)[:8]
            lse_ref[0, 8:] = jnp.zeros((8, QB), F32)

        @pl.when(active != 0)
        def _():
            mixed_two, lse_two = one(query, lambda i: m_ref[i, 2], second, first)
            o_ref[0] = jnp.where(lane < HD, mixed_two, mixed).astype(BF16)
            lse_ref[0, :8] = jnp.transpose(lse)[:8]
            lse_ref[0, 8:] = jnp.transpose(lse_two)[HD : HD + 8]


def o_block(causal):
    if causal:
        return pl.BlockSpec((1, QB, LANES), lambda i, b: (i // 2, 0, 0))
    return pl.BlockSpec((1, QB, LANES), lambda i, b: (i // 2, i % 2, 0))


def attend(causal, bounds, messages, segcol, segrow):
    rows = segcol.shape[0]
    blocks = rows // QB
    heads = 1 if causal else 2
    o_shape = (4, QB if causal else KB, LANES)
    return pl.pallas_call(
        functools.partial(attend_kernel, causal),
        grid_spec=pltpu.PrefetchScalarGridSpec(
            num_scalar_prefetch=1,
            grid=(blocks,),
            in_specs=[
                pl.BlockSpec(messages.shape, lambda i, b: (0,) * messages.ndim),
                pl.BlockSpec((QB, 1), lambda i, b: (i, 0)),
                pl.BlockSpec((1, rows), lambda i, b: (0, 0)),
            ],
            out_specs=[o_block(causal), pl.BlockSpec((1, 16, QB), lambda i, b: (i, 0, 0))],
        ),
        out_shape=[
            jax.ShapeDtypeStruct(o_shape, BF16),
            jax.ShapeDtypeStruct((blocks, 16, QB), F32),
        ],
        cost_estimate=pl.CostEstimate(
            flops=heads * 4 * rows * rows * LANES,
            bytes_accessed=6 * rows * LANES,
            transcendentals=heads * rows * rows,
        ),
        name="attend_causal" if causal else "attend_full",
    )(bounds, messages, segcol, segrow)


def attend_back_kernel(
    causal, bounds, m_ref, do_ref, o_ref, lse_ref, segcol_ref, segrow_ref, out_ref, acc_ref
):
    block = pl.program_id(0)
    low, high, active = bounds[0, block], bounds[1, block], bounds[2, block]
    source, half = block // 2, block % 2
    first, second = lane_marks()
    lane = lax.broadcasted_iota(jnp.int32, (QB, LANES), 1)

    @pl.when(block == 0)
    def _():
        acc_ref[...] = jnp.zeros_like(acc_ref)

    seg_query = segrow_ref[:, pl.ds(pl.multiple_of(block * QB, QB), QB)]

    def one(query, grad_o, load, which, own, other, lse, delta):
        query_own = query * own
        grad_own = grad_o * other

        def step(index, grad_query):
            start = pl.multiple_of(index * KB, KB)
            keys = load(index)
            scores = dot(keys, query_own, ((1,), (1,)))
            ok = segcol_ref[pl.ds(start, KB), :] == seg_query
            if causal:
                key_pos = start + lax.broadcasted_iota(jnp.int32, (KB, QB), 0)
                query_pos = block * QB + lax.broadcasted_iota(jnp.int32, (KB, QB), 1)
                ok = jnp.logical_and(ok, key_pos <= query_pos)
            weights = jnp.where(ok, jnp.exp(scores - lse), 0.0)
            grad_weights = dot(keys, grad_own, ((1,), (1,)))
            grad_scores = (weights * (grad_weights - delta)).astype(BF16)
            acc_ref[which, pl.ds(start, KB), :] += dot(grad_scores, query_own) + dot(
                weights.astype(BF16), grad_own
            )
            return grad_query + dot(grad_scores, keys, ((0,), (0,)))

        return lax.fori_loop(low, high, step, jnp.zeros((QB, LANES), F32))

    grad_o = do_ref[0].astype(F32)
    mixed = o_ref[0].astype(F32)
    if causal:
        grad_o = turn(grad_o, 1 - half)
        product = jnp.transpose(grad_o * turn(mixed, 1 - half))
        query = turn(m_ref[source, :QB].astype(F32), half).astype(BF16)
        grad_query = one(
            query,
            grad_o.astype(BF16),
            lambda i: m_ref[i, QB:],
            0,
            first,
            second,
            lse_ref[0, :1],
            jnp.sum(product[HD:], axis=0, keepdims=True),
        )
        grad_query = turn(grad_query * 0.125, half).astype(BF16)

        @pl.when(half == 0)
        def _():
            out_ref[source, :QB] = grad_query

        @pl.when(half != 0)
        def _():
            out_ref[source, :QB] = jnp.where(lane < HD, out_ref[source, :QB], grad_query)
    else:
        product = jnp.transpose(grad_o * mixed)
        rows = pl.ds(pl.multiple_of(half * QB, QB), QB)
        query = m_ref[source, 0, rows]
        grad_query = one(
            query,
            do_ref[0],
            lambda i: m_ref[i, 1],
            0,
            first,
            second,
            lse_ref[0, :1],
            jnp.sum(product[HD:], axis=0, keepdims=True),
        )

        @pl.when(active == 0)
        def _():
            out_ref[source, 0, rows] = (grad_query * 0.125).astype(BF16)

        @pl.when(active != 0)
        def _():
            grad_two = one(
                query,
                do_ref[0],
                lambda i: m_ref[i, 2],
                1,
                second,
                first,
                lse_ref[0, 8:9],
                jnp.sum(product[:HD], axis=0, keepdims=True),
            )
            out_ref[source, 0, rows] = (
                jnp.where(lane < HD, grad_query, grad_two) * 0.125
            ).astype(BF16)

    @pl.when(block == pl.num_programs(0) - 1)
    def _():
        for index in range(4):
            keys = slice(index * KB, (index + 1) * KB)
            if causal:
                out_ref[index, QB:] = acc_ref[0, keys].astype(BF16)
            else:
                out_ref[index, 1] = acc_ref[0, keys].astype(BF16)
                out_ref[index, 2] = acc_ref[1, keys].astype(BF16)


def attend_back(causal, bounds, messages, do, o, lse, segcol, segrow):
    rows = segcol.shape[0]
    blocks = rows // QB
    heads = 1 if causal else 2
    whole = pl.BlockSpec(messages.shape, lambda i, b: (0,) * messages.ndim)
    return pl.pallas_call(
        functools.partial(attend_back_kernel, causal),
        grid_spec=pltpu.PrefetchScalarGridSpec(
            num_scalar_prefetch=1,
            grid=(blocks,),
            in_specs=[
                whole,
                o_block(causal),
                o_block(causal),
                pl.BlockSpec((1, 16, QB), lambda i, b: (i, 0, 0)),
                pl.BlockSpec((rows, 1), lambda i, b: (0, 0)),
                pl.BlockSpec((1, rows), lambda i, b: (0, 0)),
            ],
            out_specs=whole,
            scratch_shapes=[pltpu.VMEM((heads, rows, LANES), F32)],
        ),
        out_shape=jax.ShapeDtypeStruct(messages.shape, BF16),
        cost_estimate=pl.CostEstimate(
            flops=heads * 10 * rows * rows * LANES,
            bytes_accessed=12 * rows * LANES,
            transcendentals=heads * rows * rows,
        ),
        name="attend_back_causal" if causal else "attend_back_full",
    )(bounds, messages, do, o, lse, segcol, segrow)


def block_bounds(seg, causal):
    blocks = seg.reshape(-1, QB)
    begin = jnp.sum(seg[None, :] < blocks[:, :1], axis=1, dtype=jnp.int32)
    end = jnp.sum(seg[None, :] <= blocks[:, -1:], axis=1, dtype=jnp.int32)
    if causal:
        end = jnp.minimum(end, (jnp.arange(blocks.shape[0], dtype=jnp.int32) + 1) * QB)
    half = lax.axis_index(CTX) % 2
    count = blocks.shape[0]
    active = (jnp.arange(count, dtype=jnp.int32) // (count // 2) == half).astype(jnp.int32)
    return jnp.stack([begin // KB, (end + KB - 1) // KB, active])


class Bag:
    pass


def partners():
    at = Bag()
    group, here, core = lax.axis_index(FSDP), lax.axis_index(CTX), lax.axis_index(TP)
    at.group, at.here = group, here
    at.group_x = group + 1 - 2 * (group % 2)
    at.group_y = group + 2 - 4 * (group // 2)
    at.group_far = 3 - group
    at.here_low, at.here_high = here % 2, here // 2
    at.ctx = (here, here + 1 - 2 * (here % 2), here + 2 - 4 * (here // 2), 3 - here)
    at.to_x, at.to_y, at.to_far = ({FSDP: g} for g in (at.group_x, at.group_y, at.group_far))
    at.to_ctx = [{CTX: c} for c in at.ctx]
    at.to_core = {TP: 1 - core}
    return at


def meet(devices):
    barrier = pltpu.get_barrier_semaphore()
    for device in devices:
        pl.semaphore_signal(barrier, inc=1, device_id=device, device_id_type=MESH)
    pl.semaphore_wait(barrier, len(devices))


class Copies:
    def __init__(self, send_sems, recv_sems, local_sems):
        self.sems = (send_sems, recv_sems, local_sems)
        self.used = [0, 0]

    def remote(self, src, dst, device):
        index = self.used[0]
        self.used[0] += 1
        copy = pltpu.make_async_remote_copy(
            src_ref=src,
            dst_ref=dst,
            send_sem=self.sems[0].at[index],
            recv_sem=self.sems[1].at[index],
            device_id=device,
            device_id_type=MESH,
        )
        copy.start()
        return copy

    def local(self, src, dst):
        index = self.used[1]
        self.used[1] += 1
        copy = pltpu.make_async_copy(src, dst, self.sems[2].at[index])
        copy.start()
        return copy


def copy_sems(remote, local):
    return [
        pltpu.SemaphoreType.DMA((remote,)),
        pltpu.SemaphoreType.DMA((remote,)),
        pltpu.SemaphoreType.DMA((local,)),
    ]


class Gather:
    def __init__(self, copies, at, src, dst):
        self.copies, self.at, self.dst = copies, at, dst
        self.rows = src.shape[-2]
        own = self.part(at.group, 0, self.rows)
        self.own = copies.local(src, own)
        self.to_x = copies.remote(src, own, at.to_x)
        self.to_y = copies.remote(src, own, at.to_y)

    def part(self, owner, offset, size):
        rows = pl.ds(pl.multiple_of(owner * self.rows + offset, 8), size)
        return self.dst.at[:, rows, :] if len(self.dst.shape) == 3 else self.dst.at[rows, :]

    def forward(self):
        half = self.rows // 2
        self.to_x.wait_recv()
        self.to_y.wait_recv()
        top = self.part(self.at.group_y, 0, half)
        low = self.part(self.at.group_x, half, half)
        self.far_x = self.copies.remote(top, top, self.at.to_x)
        self.far_y = self.copies.remote(low, low, self.at.to_y)

    def arrived(self):
        self.own.wait()
        self.far_x.wait_recv()
        self.far_y.wait_recv()

    def sent(self):
        for copy in (self.to_x, self.to_y, self.far_x, self.far_y):
            copy.wait_send()


def normalise(rows):
    mean = jnp.mean(rows, axis=-1, keepdims=True)
    centred = rows - mean
    inv = lax.rsqrt(jnp.mean(centred * centred, axis=-1, keepdims=True) + 1e-05)
    return centred * inv, inv


def lane_pair(low, high):
    lane = lax.broadcasted_iota(jnp.int32, low[0].shape, 1)
    left = low[0] if low[1] == 0 else pltpu.roll(low[0], HD, 1)
    right = high[0] if high[1] == 1 else pltpu.roll(high[0], HD, 1)
    return jnp.where(lane < HD, left, right)


def head_tile(ref, start, index, rows=slice(None)):
    first = start + (index // 2) * LANES
    return ref[rows, first : first + LANES], index % 2


def write_messages(qkv, out, heads):
    width = heads * HD
    tokens = qkv.shape[0]
    for c in range(4):
        if heads == 4:
            half = tokens // 2
            out[c, :half] = lane_pair(
                head_tile(qkv, 0, c, slice(0, half)), head_tile(qkv, 0, c, slice(half, None))
            ).astype(BF16)
            out[c, half:] = lane_pair(
                head_tile(qkv, width, c), head_tile(qkv, 2 * width, c)
            ).astype(BF16)
        else:
            e = 4 + c // 2
            out[c, 0] = lane_pair(head_tile(qkv, 0, c), head_tile(qkv, 0, e)).astype(BF16)
            out[c, 1] = lane_pair(
                head_tile(qkv, width, c), head_tile(qkv, 2 * width, c)
            ).astype(BF16)
            out[c, 2] = lane_pair(
                head_tile(qkv, 2 * width, e), head_tile(qkv, width, e)
            ).astype(BF16)


def front_stream_sizes(width, heads, tokens):
    part = (tokens // 2 + tokens, LANES) if heads == 4 else (3, tokens, LANES)
    return (4,) + part


def first_rows(x_ref, small_ref, weight_ref, first_ref, qkv_ref, step):
    width = weight_ref.shape[2]
    rows = slice(step * 256, step * 256 + 256)
    normed, _ = normalise(x_ref[rows, :].astype(F32))
    first = (normed * small_ref[0:1] + small_ref[2:3]).astype(BF16)
    first_ref[:, rows] = jnp.transpose(first)
    bias = small_ref[6:7]
    qkv_ref[rows, :width] = (dot(first, weight_ref[0]) + bias[:, :width]) * 0.125
    qkv_ref[rows, width : 2 * width] = dot(first, weight_ref[1])
    qkv_ref[rows, 2 * width :] = dot(first, weight_ref[2]) + bias[:, width : 2 * width]


def front_kernel(*refs):
    at = partners()
    n = 6
    ins = [refs[:n], refs[n : 2 * n]]
    refs = refs[2 * n :]
    n = 7
    outs = [refs[:n], refs[n : 2 * n]]
    refs = refs[2 * n :]
    n = 5
    scratch = [refs[:n], refs[n : 2 * n]]
    copies = Copies(*refs[2 * n :])
    meet(
        [at.to_x, at.to_y, at.to_far]
        + at.to_ctx[1:]
    )
    small_copies, first_gathers = [], []
    for (x, small, qkv, up, down, proj), out, (small_in, *_) in zip(ins, outs, scratch):
        small_copies.append(
            [
                copies.remote(small, small_in.at[i], device)
                for i, device in enumerate((at.to_x, at.to_y, at.to_far))
            ]
        )
        first_gathers.append(Gather(copies, at, qkv, out[0]))
    for (x, small, qkv, up, down, proj), (_, _, _, down_t, proj_t) in zip(ins, scratch):
        if down.shape[0] > down.shape[1]:
            down_t[...] = jnp.transpose(down[...])
            proj_t[...] = jnp.transpose(proj[...])
    rest_gathers = []
    for gather in first_gathers:
        gather.forward()
    for (x, small, qkv, up, down, proj), out, (_, _, _, down_t, proj_t) in zip(ins, outs, scratch):
        flip = down.shape[0] > down.shape[1]
        for piece, full in zip((proj_t if flip else proj, up, down_t if flip else down), out[4:]):
            rest_gathers.append(Gather(copies, at, piece, full))
    sends = []
    for which in (0, 1):
        x, small = ins[which][:2]
        weight, small_full, first, messages = outs[which][:4]
        small_in, qkv, mine, _, _ = scratch[which]
        for copy in small_copies[which]:
            copy.wait_recv()
        small_full[...] = small[...] + small_in[0] + small_in[1] + small_in[2]
        first_gathers[which].arrived()
        for step in range(x.shape[0] // 256):
            first_rows(x, small_full, weight, first, qkv, step)
        heads = weight.shape[2] // HD
        write_messages(qkv, mine, heads)
        sends.append(copies.local(mine.at[at.here], messages.at[at.here]))
        for other in at.ctx[1:]:
            sends.append(
                copies.remote(mine.at[other], messages.at[at.here], {CTX: other})
            )
        for gather in rest_gathers[3 * which : 3 * which + 3]:
            gather.forward()
    for gather in rest_gathers:
        gather.arrived()
    for gather in first_gathers + rest_gathers:
        gather.sent()
    for copy in sends:
        copy.wait()
    for copy in small_copies[0] + small_copies[1]:
        copy.wait_send()


def front(streams):
    vmem, hbm = pl.BlockSpec(memory_space=pltpu.VMEM), pl.BlockSpec(memory_space=pl.ANY)
    out_shape, out_specs, scratch = [], [], []
    for x, small, qkv, up, down, proj in streams:
        tokens, width = x.shape
        heads = qkv.shape[2] // HD
        messages = front_stream_sizes(width, heads, tokens)
        hidden = up.shape[1]
        out_shape += [
            jax.ShapeDtypeStruct((3, width, heads * HD), BF16),
            jax.ShapeDtypeStruct(small.shape, F32),
            jax.ShapeDtypeStruct((width, tokens), BF16),
            jax.ShapeDtypeStruct(messages, BF16),
            jax.ShapeDtypeStruct((width, heads * HD), BF16),
            jax.ShapeDtypeStruct((width, hidden), BF16),
            jax.ShapeDtypeStruct((width, hidden), BF16),
        ]
        out_specs += [vmem, vmem, vmem, hbm, hbm, hbm, hbm]
        scratch += [
            pltpu.VMEM((3,) + small.shape, F32),
            pltpu.VMEM((tokens, 3 * heads * HD), F32),
            pltpu.VMEM(messages, BF16),
            pltpu.VMEM((width // 4, hidden), BF16),
            pltpu.VMEM((width // 4, heads * HD), BF16),
        ]
    results = pl.pallas_call(
        front_kernel,
        out_shape=out_shape,
        in_specs=[vmem] * 12,
        out_specs=out_specs,
        scratch_shapes=scratch + copy_sems(2 * (3 + 4 * 4 + 3), 2 * 5),
        compiler_params=pltpu.CompilerParams(
            collective_id=0, has_side_effects=True, vmem_limit_bytes=60 << 20
        ),
        name="front",
    )(*streams[0], *streams[1])
    return results[:7], results[7:]


def place_small(gains, shifts, head_bias):
    group = lax.axis_index(FSDP)
    width = 4 * gains.shape[1]

    def spread(array, columns):
        out = jnp.zeros((array.shape[0], columns), F32)
        return lax.dynamic_update_slice_in_dim(
            out, array.astype(F32), group * array.shape[1], 1
        )

    bias = spread(head_bias, 4 * head_bias.shape[1]).reshape(-1, width)
    rows = jnp.concatenate([spread(gains, width), spread(shifts, width), bias])
    return jnp.pad(rows, ((0, 16 - rows.shape[0]), (0, 0)))


def chunks(tokens, size=256):
    return [slice(start, start + size) for start in range(0, tokens, size)]


def as_f32(ref, index, rows=slice(None)):
    return ref[index, rows].astype(F32)


def take_mixed(got, mixed, at, heads):
    tokens = mixed.shape[0]
    if heads == 4:
        half = tokens // 2
        for tile in range(2):
            cols = slice(tile * LANES, (tile + 1) * LANES)
            one, two = as_f32(got, 2 * tile), as_f32(got, 2 * tile + 1)
            mixed[:half, cols] = lane_pair((one, 0), (two, 0)).astype(BF16)
            mixed[half:, cols] = lane_pair((one, 1), (two, 1)).astype(BF16)
        return
    for tile in range(2):
        cols = slice(tile * LANES, (tile + 1) * LANES)
        mixed[:, cols] = lane_pair(
            (as_f32(got, 2 * tile), 1), (as_f32(got, 2 * tile + 1), 1)
        ).astype(BF16)
    part = at.here // 2
    mixed[:, 2 * LANES :] = lane_pair((as_f32(got, part), 0), (as_f32(got, part + 2), 0)).astype(BF16)


def write_grad_o(grad, out, heads):
    tokens = grad.shape[0]
    half = tokens // 2
    for c in range(4):
        if heads == 4:
            out[c] = lane_pair(
                head_tile(grad, 0, c, slice(0, half)), head_tile(grad, 0, c, slice(half, None))
            ).astype(BF16)
        else:
            out[c] = lane_pair(head_tile(grad, 0, 4 + c // 2), head_tile(grad, 0, c)).astype(BF16)


def send_blocks(copies, at, mine, out):
    done = [copies.local(mine.at[at.here], out.at[at.here])]
    for other in at.ctx[1:]:
        done.append(copies.remote(mine.at[other], out.at[at.here], {CTX: other}))
    return done


def middle_kernel(*refs):
    at = partners()
    n = 7
    ins = [refs[:n], refs[n : 2 * n]]
    refs = refs[2 * n :]
    n = 5
    outs = [refs[:n], refs[n : 2 * n]]
    refs = refs[2 * n :]
    n = 16
    scratch = [refs[:n], refs[n : 2 * n]]
    copies = Copies(*refs[2 * n :])
    other_core = at.to_core
    meet(at.to_ctx[1:] + [other_core])
    streams = []
    for (o, x, dy, small, proj_in, up_in, down_in), out, own in zip(ins, outs, scratch):
        s = Bag()
        s.o, s.x, s.dy, s.small = o, x, dy, small
        s.y, s.dmid, s.do_out, s.rest, s.sums = out
        (
            s.proj, s.up, s.down, s.o_in, s.mixed, s.part, s.part_in, s.mid, s.first_t, s.dy_t,
            s.act, s.dz, s.grad, s.grad_in, s.do, s.do_mine,
        ) = own
        s.heads = proj_in.shape[1] // HD
        s.o_done = send_blocks(copies, at, o, s.o_in)
        s.proj_done = copies.local(proj_in, s.proj)
        streams.append(s)
    for s, (o, x, dy, small, proj_in, up_in, down_in) in zip(streams, ins):
        s.rest_done = [copies.local(up_in, s.up), copies.local(down_in, s.down)]
        s.sums[...] = jnp.zeros_like(s.sums)
        for rows in chunks(dy.shape[0]):
            s.dy_t[:, rows] = jnp.transpose(dy[rows, :])
    for s in streams:
        tokens, width = s.x.shape
        for copy in s.o_done:
            copy.wait()
        take_mixed(s.o_in, s.mixed, at, s.heads)
        s.proj_done.wait()
        for cols in chunks(width):
            s.part[:, cols] = dot(s.mixed[...], s.proj[cols, :], ((1,), (1,)))
        s.part_done = copies.remote(s.part, s.part_in, other_core)
    for s in streams:
        tokens, width = s.x.shape
        hidden = s.up.shape[1]
        small, mid, first_t, dy_t = s.small, s.mid, s.first_t, s.dy_t
        s.part_done.wait()
        for rows in chunks(tokens):
            middle = (
                s.x[rows, :].astype(F32) + s.part[rows, :] + s.part_in[rows, :] + small[3:4]
            )
            mid[rows, :] = middle
            normed, _ = normalise(middle)
            first_t[:, rows] = jnp.transpose((normed * small[1:2] + small[4:5]).astype(BF16))
        for copy in s.rest_done:
            copy.wait()
        act, dz = s.act, s.dz

        def tile(index, carry, s=s, act=act, dz=dz, first_t=first_t, dy_t=dy_t, small=small, tokens=tokens, width=width, hidden=hidden):
            cols = pl.ds(pl.multiple_of(index * 256, 256), 256)
            up, down = s.up[:, cols], s.down[:, cols]
            per_row = width // 256
            own = s.proj.shape[1]
            up_cols = pl.ds(pl.multiple_of(own + index * 256, LANES), 256)
            down_cols = pl.ds(pl.multiple_of(own + hidden + index * 256, LANES), 256)
            bias = small[pl.ds(7 + index // per_row, 1), pl.ds(pl.multiple_of((index % per_row) * 256, 256), 256)]
            total = jnp.zeros((1, 256), F32)
            for rows in chunks(tokens):
                z = dot(first_t[:, rows], up, ((0,), (0,))) + bias
                sg = jax.nn.sigmoid(1.702 * z)
                zs = z * sg
                act[rows, cols] = zs.astype(BF16)
                grad = dot(s.dy[rows, :], down)
                low = (grad * (sg + 1.702 * zs * (1.0 - sg))).astype(BF16)
                dz[rows, cols] = low
                total = total + jnp.sum(low.astype(F32), axis=0, keepdims=True)
            s.sums[pl.ds(7 + index // per_row, 1), pl.ds(pl.multiple_of((index % per_row) * 256, 256), 256)] = total
            s.rest[:, up_cols] = dot(first_t[...], dz[:, cols]).astype(BF16)
            s.rest[:, down_cols] = dot(dy_t[...], act[:, cols]).astype(BF16)
            return carry

        lax.fori_loop(0, hidden // 256, tile, 0)
        grad = s.grad
        for cols in chunks(width):
            grad[0, :, cols] = dot(dz[...], s.up[cols, :], ((1,), (1,)))
        s.grad_done = copies.remote(grad.at[0], s.grad_in.at[0], other_core)
        for cols in chunks(width):
            grad[1, :, cols] = dot(act[...], s.down[cols, :], ((1,), (1,)))
        s.y_done = copies.remote(grad.at[1], s.grad_in.at[1], other_core)
    for s in streams:
        tokens, width = s.x.shape
        small, sums = s.small, s.sums
        s.grad_done.wait()
        for rows in chunks(tokens):
            normed, inv = normalise(s.mid[rows, :])
            second = s.grad[0, rows, :] + s.grad_in[0, rows, :]
            scaled = second * small[1:2]
            dy = s.dy[rows, :].astype(F32)
            dmid = dy + inv * (
                scaled
                - jnp.mean(scaled, axis=-1, keepdims=True)
                - normed * jnp.mean(scaled * normed, axis=-1, keepdims=True)
            )
            s.dmid[rows, :] = dmid
            sums[1:2] += jnp.sum(second * normed, axis=0, keepdims=True)
            sums[3:4] += jnp.sum(dmid, axis=0, keepdims=True)
            sums[4:5] += jnp.sum(second, axis=0, keepdims=True)
            sums[5:6] += jnp.sum(dy, axis=0, keepdims=True)
            low = dmid.astype(BF16)
            s.first_t[:, rows] = jnp.transpose(low)
            s.do[rows, :] = dot(low, s.proj[...])
        write_grad_o(s.do, s.do_mine, s.heads)
        s.do_done = send_blocks(copies, at, s.do_mine, s.do_out)
        s.rest[:, : s.proj.shape[1]] = dot(s.first_t[...], s.mixed[...]).astype(BF16)
        s.y_done.wait()
        for rows in chunks(tokens):
            s.y[rows, :] = (
                s.mid[rows, :] + s.grad[1, rows, :] + s.grad_in[1, rows, :] + small[5:6]
            ).astype(BF16)
    for s in streams:
        for copy in s.do_done:
            copy.wait()


def middle(streams):
    vmem, hbm = pl.BlockSpec(memory_space=pltpu.VMEM), pl.BlockSpec(memory_space=pl.ANY)
    out_shape, out_specs, scratch = [], [], []
    for o, x, dy, small, proj, up, down in streams:
        tokens, width = x.shape
        hidden, own = up.shape[1], proj.shape[1]
        out_shape += [
            jax.ShapeDtypeStruct((tokens, width), BF16),
            jax.ShapeDtypeStruct((tokens, width), F32),
            jax.ShapeDtypeStruct(o.shape, BF16),
            jax.ShapeDtypeStruct((width, own + 2 * hidden), BF16),
            jax.ShapeDtypeStruct(small.shape, F32),
        ]
        out_specs += [vmem, vmem, hbm, vmem, vmem]
        scratch += [
            pltpu.VMEM(proj.shape, BF16),
            pltpu.VMEM(up.shape, BF16),
            pltpu.VMEM(down.shape, BF16),
            pltpu.VMEM(o.shape, BF16),
            pltpu.VMEM((tokens, own), BF16),
            pltpu.VMEM((tokens, width), F32),
            pltpu.VMEM((tokens, width), F32),
            pltpu.VMEM((tokens, width), F32),
            pltpu.VMEM((width, tokens), BF16),
            pltpu.VMEM((width, tokens), BF16),
            pltpu.VMEM((tokens, hidden), BF16),
            pltpu.VMEM((tokens, hidden), BF16),
            pltpu.VMEM((2, tokens, width), F32),
            pltpu.VMEM((2, tokens, width), F32),
            pltpu.VMEM((tokens, own), F32),
            pltpu.VMEM(o.shape, BF16),
        ]
    results = pl.pallas_call(
        middle_kernel,
        out_shape=out_shape,
        in_specs=([vmem] * 4 + [hbm] * 3) * 2,
        out_specs=out_specs,
        scratch_shapes=scratch + copy_sems(2 * 9, 2 * 5),
        compiler_params=pltpu.CompilerParams(
            collective_id=1, has_side_effects=True, vmem_limit_bytes=63 << 20
        ),
        name="middle",
    )(*streams[0], *streams[1])
    return results[:5], results[5:]


STEP = 384


def by_columns(columns, body):
    def one(index, carry):
        body(pl.ds(pl.multiple_of(index * STEP, STEP), STEP))
        return carry

    lax.fori_loop(0, columns // STEP, one, 0)


class Reduce:
    BUFFERS = 11

    def __init__(self, copies, at, src, buffers):
        self.copies, self.at = copies, at
        (
            self.own, self.pass_top, self.pass_low, self.in_x, self.in_y, self.in_top, self.in_low,
            self.total, self.half_out, self.quarter_out, self.final,
        ) = buffers[: self.BUFFERS]
        self.half_in, self.quarter_in = buffers[self.BUFFERS :]
        rows, self.columns = self.final.shape
        self.rows, half = rows, rows // 2
        self.half = half

        def block(owner, offset, size):
            return src.at[pl.ds(pl.multiple_of(owner * rows + offset, 8), size), :]

        self.loads = [
            copies.local(block(at.group_y, 0, half), self.pass_top),
            copies.local(block(at.group_x, half, half), self.pass_low),
            copies.local(block(at.group, 0, rows), self.own),
        ]
        self.first = [
            copies.remote(block(at.group_far, 0, half), self.in_x.at[1], at.to_x),
            copies.remote(block(at.group_far, half, half), self.in_y.at[1], at.to_y),
            copies.remote(block(at.group_x, 0, half), self.in_x.at[0], at.to_x),
            copies.remote(block(at.group_y, half, half), self.in_y.at[0], at.to_y),
        ]

    def cross(self):
        self.loads[0].wait()
        self.first[0].wait_recv()

        def top(cols):
            self.pass_top[:, cols] = (
                self.pass_top[:, cols].astype(F32) + self.in_x[1, :, cols].astype(F32)
            ).astype(BF16)

        by_columns(self.columns, top)
        self.second = [self.copies.remote(self.pass_top, self.in_top, self.at.to_y)]
        self.loads[1].wait()
        self.first[1].wait_recv()

        def low(cols):
            self.pass_low[:, cols] = (
                self.pass_low[:, cols].astype(F32) + self.in_y[1, :, cols].astype(F32)
            ).astype(BF16)

        by_columns(self.columns, low)
        self.second.append(self.copies.remote(self.pass_low, self.in_low, self.at.to_x))

    def along(self):
        half = self.half
        self.loads[2].wait()
        self.first[2].wait_recv()
        self.first[3].wait_recv()
        self.second[0].wait_recv()
        self.second[1].wait_recv()

        def plane(cols):
            self.total[:half, cols] = (
                self.own[:half, cols].astype(F32)
                + self.in_x[0, :, cols].astype(F32)
                + self.in_top[:, cols].astype(F32)
            )
            self.total[half:, cols] = (
                self.own[half:, cols].astype(F32)
                + self.in_y[0, :, cols].astype(F32)
                + self.in_low[:, cols].astype(F32)
            )

        by_columns(self.columns, plane)
        self.keep = pl.ds(pl.multiple_of(self.at.here_low * half, 8), half)
        give = pl.ds(pl.multiple_of((1 - self.at.here_low) * half, 8), half)

        def send(cols):
            self.half_out[:, cols] = self.total[give, cols].astype(BF16)

        by_columns(self.columns, send)
        self.third = self.copies.remote(self.half_out, self.half_in, self.at.to_ctx[1])

    def along_far(self):
        quarter = self.half // 2
        self.third.wait_recv()
        base = self.at.here_low * self.half
        mine = pl.ds(pl.multiple_of(self.at.here_high * quarter, 8), quarter)
        other = pl.ds(pl.multiple_of((1 - self.at.here_high) * quarter, 8), quarter)
        self.keep_low = pl.ds(pl.multiple_of(base + self.at.here_high * quarter, 8), quarter)
        give = pl.ds(pl.multiple_of(base + (1 - self.at.here_high) * quarter, 8), quarter)

        def send(cols):
            self.quarter_out[:, cols] = (
                self.total[give, cols] + self.half_in[other, cols].astype(F32)
            ).astype(BF16)

        by_columns(self.columns, send)
        self.fourth = self.copies.remote(self.quarter_out, self.quarter_in, self.at.to_ctx[2])
        self.mine = mine

    def back_far(self):
        self.fourth.wait_recv()

        def add(cols):
            self.final[self.keep_low, cols] = (
                self.total[self.keep_low, cols]
                + self.half_in[self.mine, cols].astype(F32)
                + self.quarter_in[:, cols].astype(F32)
            ).astype(BF16)

        by_columns(self.columns, add)
        rows = self.final.at[self.keep_low, :]
        self.fifth = self.copies.remote(rows, rows, self.at.to_ctx[2])

    def back_near(self):
        self.fifth.wait_recv()
        rows = self.final.at[self.keep, :]
        self.sixth = self.copies.remote(rows, rows, self.at.to_ctx[1])

    def finish(self):
        self.sixth.wait_recv()
        for copy in self.first + self.second + [self.third, self.fourth, self.fifth, self.sixth]:
            copy.wait_send()

    @staticmethod
    def scratch(rows, columns):
        half, quarter = rows // 2, rows // 4
        return [
            pltpu.VMEM((rows, columns), BF16),
            pltpu.VMEM((half, columns), BF16),
            pltpu.VMEM((half, columns), BF16),
            pltpu.VMEM((2, half, columns), BF16),
            pltpu.VMEM((2, half, columns), BF16),
            pltpu.VMEM((half, columns), BF16),
            pltpu.VMEM((half, columns), BF16),
            pltpu.VMEM((rows, columns), F32),
            pltpu.VMEM((half, columns), BF16),
            pltpu.VMEM((quarter, columns), BF16),
        ]

    @staticmethod
    def scratch_in(rows, columns):
        return [pltpu.VMEM((rows // 2, columns), BF16), pltpu.VMEM((rows // 4, columns), BF16)]


def take_dqkv(got, out, at, heads):
    tokens, width = out.shape[0], heads * HD

    def put(which, tile, rows, low, high):
        start = which * width + tile * LANES
        out[rows, start : start + LANES] = lane_pair(low, high).astype(BF16)

    every = slice(None)
    if heads == 4:
        half = tokens // 2
        top, low, keys = slice(0, half), slice(half, tokens), slice(half, half + tokens)
        for tile in range(2):
            one, two = 2 * tile, 2 * tile + 1
            for side, rows in ((0, top), (1, low)):
                put(0, tile, rows, (as_f32(got, one, top), side), (as_f32(got, two, top), side))
            for which in (1, 2):
                side = which - 1
                put(which, tile, every, (as_f32(got, one, keys), side), (as_f32(got, two, keys), side))
        return

    def part(position, index):
        return got[position, index].astype(F32)

    for tile in range(2):
        one, two = 2 * tile, 2 * tile + 1
        put(0, tile, every, (part(one, 0), 0), (part(two, 0), 0))
        put(1, tile, every, (part(one, 1), 0), (part(two, 1), 0))
        put(2, tile, every, (part(one, 1), 1), (part(two, 1), 1))
    put(0, 2, every, (part(at.here_high, 0), 1), (part(at.here_high + 2, 0), 1))
    one, two = part(0, 2) + part(1, 2), part(2, 2) + part(3, 2)
    put(1, 2, every, (one, 1), (two, 1))
    put(2, 2, every, (one, 0), (two, 0))


LAST_IN, LAST_OUT, LAST_SCRATCH = 8, 4, 9


def last_kernel(*refs):
    at = partners()
    ins = [refs[:LAST_IN], refs[LAST_IN : 2 * LAST_IN]]
    refs = refs[2 * LAST_IN :]
    outs = [refs[:LAST_OUT], refs[LAST_OUT : 2 * LAST_OUT]]
    refs = refs[2 * LAST_OUT :]
    count = LAST_SCRATCH + 2 * 12
    scratch = [refs[:count], refs[count : 2 * count]]
    copies = Copies(*refs[2 * count :])
    meet([at.to_x, at.to_y] + at.to_ctx[1:] + [at.to_core])
    streams = []
    for in_refs, out_refs, own in zip(ins, outs, scratch):
        s = Bag()
        s.back, s.first_in, s.x_in, s.small, s.weight_in, s.dmid_in, s.rest, s.sums_in = in_refs
        s.grad_rows, s.sums, rest_final, qkv_final = out_refs
        (
            s.got, s.dqkv, s.weight, s.first, s.x, s.dmid, s.part, s.part_in, s.g_qkv,
        ) = own[:LAST_SCRATCH]
        rest_buffers = list(own[LAST_SCRATCH : LAST_SCRATCH + 12])
        s.qkv_buffers = list(own[LAST_SCRATCH + 12 :])
        rest_buffers.insert(10, rest_final)
        s.qkv_buffers.insert(10, qkv_final)
        s.heads = s.weight.shape[2] // HD
        s.back_done = send_blocks(copies, at, s.back, s.got)
        s.loads = [
            copies.local(src, dst)
            for src, dst in (
                (s.weight_in, s.weight), (s.first_in, s.first), (s.x_in, s.x), (s.dmid_in, s.dmid),
            )
        ]
        s.rest_buffers = rest_buffers
        streams.append(s)
    for s in streams:
        s.reduce_rest = Reduce(copies, at, s.rest, s.rest_buffers)
    for s in streams:
        tokens, width = s.x.shape
        own = s.heads * HD
        for copy in s.back_done:
            copy.wait()
        for copy in s.loads:
            copy.wait()
        take_dqkv(s.got, s.dqkv, at, s.heads)
        for cols in chunks(width):
            total = dot(s.dqkv[:, :own], s.weight[0, cols, :], ((1,), (1,)))
            total = total + dot(s.dqkv[:, own : 2 * own], s.weight[1, cols, :], ((1,), (1,)))
            s.part[:, cols] = total + dot(s.dqkv[:, 2 * own :], s.weight[2, cols, :], ((1,), (1,)))
        s.part_done = copies.remote(s.part, s.part_in, at.to_core)
        for which in range(3):
            cols = slice(which * own, (which + 1) * own)
            s.g_qkv[:, cols] = dot(s.first[...], s.dqkv[:, cols]).astype(BF16)
        s.reduce_qkv = Reduce(copies, at, s.g_qkv, s.qkv_buffers)
        s.sums[...] = s.sums_in[...]
        s.sums[6:7, :own] = jnp.sum(s.dqkv[:, :own].astype(F32), axis=0, keepdims=True)
        s.sums[6:7, own:] = jnp.sum(s.dqkv[:, 2 * own :].astype(F32), axis=0, keepdims=True)
        s.reduce_rest.cross()
    for s in streams:
        tokens, width = s.x.shape
        s.part_done.wait()
        for rows in chunks(tokens):
            normed, inv = normalise(s.x[rows, :].astype(F32))
            first = s.part[rows, :] + s.part_in[rows, :]
            scaled = first * s.small[0:1]
            s.grad_rows[rows, :] = s.dmid[rows, :] + inv * (
                scaled
                - jnp.mean(scaled, axis=-1, keepdims=True)
                - normed * jnp.mean(scaled * normed, axis=-1, keepdims=True)
            )
            s.sums[0:1] += jnp.sum(first * normed, axis=0, keepdims=True)
            s.sums[2:3] += jnp.sum(first, axis=0, keepdims=True)
        s.reduce_rest.along()
    for s in streams:
        s.reduce_qkv.cross()
    for s in streams:
        s.reduce_rest.along_far()
    for s in streams:
        s.reduce_qkv.along()
    for s in streams:
        s.reduce_rest.back_far()
    for s in streams:
        s.reduce_qkv.along_far()
    for s in streams:
        s.reduce_rest.back_near()
    for s in streams:
        s.reduce_qkv.back_far()
    for s in streams:
        s.reduce_qkv.back_near()
    for s in streams:
        s.reduce_rest.finish()
    for s in streams:
        s.reduce_qkv.finish()


def last(streams):
    vmem, hbm = pl.BlockSpec(memory_space=pltpu.VMEM), pl.BlockSpec(memory_space=pl.ANY)
    out_shape, scratch = [], []
    for back, first, x, small, weight, dmid, rest, sums in streams:
        tokens, width = x.shape
        own = weight.shape[2]
        rest_shape, qkv_shape = (width // 4, rest.shape[1]), (width // 4, 3 * own)
        out_shape += [
            jax.ShapeDtypeStruct((tokens, width), F32),
            jax.ShapeDtypeStruct(small.shape, F32),
            jax.ShapeDtypeStruct(rest_shape, BF16),
            jax.ShapeDtypeStruct(qkv_shape, BF16),
        ]
        scratch += [
            pltpu.VMEM(back.shape, BF16),
            pltpu.VMEM((tokens, 3 * own), BF16),
            pltpu.VMEM(weight.shape, BF16),
            pltpu.VMEM(first.shape, BF16),
            pltpu.VMEM((tokens, width), BF16),
            pltpu.VMEM((tokens, width), F32),
            pltpu.VMEM((tokens, width), F32),
            pltpu.VMEM((tokens, width), F32),
            pltpu.VMEM((width, 3 * own), BF16),
        ]
        for shape in (rest_shape, qkv_shape):
            scratch += Reduce.scratch(*shape) + Reduce.scratch_in(*shape)
    results = pl.pallas_call(
        last_kernel,
        out_shape=out_shape,
        in_specs=[hbm, hbm, hbm, vmem, hbm, hbm, hbm, vmem] * 2,
        out_specs=[vmem] * 8,
        scratch_shapes=scratch + copy_sems(2 * (3 + 1 + 2 * 10), 2 * (1 + 4 + 2 * 3)),
        compiler_params=pltpu.CompilerParams(
            collective_id=2, has_side_effects=True, vmem_limit_bytes=63 << 20
        ),
        name="last",
    )(*streams[0], *streams[1])
    return results[:4], results[4:]


def finish_kernel(*refs):
    ins = [refs[:3], refs[3:6]]
    outs = [refs[6:13], refs[13:]]
    for (sums, rest, qkv), (gains, shifts, bias, qkv_out, proj, up, down) in zip(ins, outs):
        gains[...] = sums[0:2]
        shifts[...] = sums[2:6]
        bias[...] = sums[6:9]
        own = qkv.shape[1] // 3
        for which in range(3):
            qkv_out[which] = qkv[:, which * own : (which + 1) * own].astype(F32)
        hidden = up.shape[1]
        up[...] = rest[:, own : own + hidden].astype(F32)
        if down.shape[0] > down.shape[1]:
            proj[...] = jnp.transpose(rest[:, :own].astype(F32))
            down[...] = jnp.transpose(rest[:, own + hidden :].astype(F32))
        else:
            proj[...] = rest[:, :own].astype(F32)
            down[...] = rest[:, own + hidden :].astype(F32)


def finish(streams):
    out_shape = []
    for sums, rest, qkv, flip in streams:
        rows, own = qkv.shape[0], qkv.shape[1] // 3
        hidden = (rest.shape[1] - own) // 2
        shapes = [(2, 4 * rows), (4, 4 * rows), (3, 4 * rows), (3, rows, own)]
        shapes += [(own, rows), (rows, hidden), (hidden, rows)] if flip else [
            (rows, own), (rows, hidden), (rows, hidden)
        ]
        out_shape += [jax.ShapeDtypeStruct(shape, F32) for shape in shapes]
    results = pl.pallas_call(finish_kernel, out_shape=out_shape, name="finish")(
        *streams[0][:3], *streams[1][:3]
    )
    return results[:7], results[7:]


def own_columns(array):
    columns = array.shape[1] // 4
    return lax.dynamic_slice_in_dim(array, lax.axis_index(FSDP) * columns, columns, 1)


def on_device(*args):
    streams = []
    for item, causal in ((args[10:], True), (args[:10], False)):
        s = Bag()
        rows, s.segrow, cotangent, gains, shifts, head_bias, s.qkv, proj, s.up, down = item
        s.causal, s.x, s.dy = causal, rows[0], cotangent[0]
        s.segcol = s.segrow.reshape(-1, 1)
        s.bounds = block_bounds(s.segrow[0], causal)
        s.small = place_small(gains, shifts, head_bias)
        s.down, s.proj = (down, proj) if causal else (down.T, proj.T)
        streams.append(s)
    started = front([(s.x, s.small, s.qkv, s.up, s.down, s.proj) for s in streams])
    for s, (weight, small, first, messages, *rest) in zip(streams, started):
        s.weight, s.small, s.first, s.messages, s.weights = weight, small, first, messages, rest
        s.o, s.lse = attend(s.causal, s.bounds, messages, s.segcol, s.segrow)
    done = middle([(s.o, s.x, s.dy, s.small, *s.weights[:1], *s.weights[1:]) for s in streams])
    for s, (y, dmid, do, rest, sums) in zip(streams, done):
        s.y, s.dmid, s.rest, s.sums = y, dmid, rest, sums
        s.back = attend_back(
            s.causal, s.bounds, s.messages, do, s.o, s.lse, s.segcol, s.segrow
        )
    ended = last(
        [(s.back, s.first, s.x, s.small, s.weight, s.dmid, s.rest, s.sums) for s in streams]
    )
    totals = reduce_small(jnp.concatenate([sums for _, sums, _, _ in ended], axis=1))
    cut = streams[0].x.shape[1]
    final = finish(
        [
            (total, rest, qkv, s.causal)
            for s, total, (_, _, rest, qkv) in zip(
                streams, (totals[:, :cut], totals[:, cut:]), ended
            )
        ]
    )
    outputs = []
    for s, (grad_rows, *_), (gains, shifts, bias, qkv, proj, up, down) in zip(streams, ended, final):
        if not s.causal:
            proj, down = proj.T, down.T
        outputs.append(
            (
                s.y[None],
                grad_rows[None],
                own_columns(gains),
                own_columns(shifts),
                own_columns(bias.reshape(1, -1)),
                qkv,
                proj,
                up,
                down,
            )
        )
    return outputs[1] + outputs[0]


def layer_stats(rows):
    row_mean = jnp.mean(rows, axis=-1, keepdims=True)
    centred = rows - row_mean
    inv_std = lax.rsqrt(jnp.mean(centred * centred, axis=-1, keepdims=True) + 1e-05)
    return (centred * inv_std, inv_std)


def norm_back(grad_normed_out, normed, inv_std, gain):
    scaled = grad_normed_out * gain
    return inv_std * (
        scaled
        - jnp.mean(scaled, axis=-1, keepdims=True)
        - normed * jnp.mean(scaled * normed, axis=-1, keepdims=True)
    )


def tensor_psum(partial_rows):
    return lax.psum(partial_rows, TP)


def any_mesh_block(
    rows_in,
    seg_row,
    cotangent,
    gains,
    shifts,
    head_bias,
    qkv_weight,
    proj_weight,
    up_weight,
    down_weight,
    causal,
):
    gain_full, shift_full, bias_full, qkv_full, proj_full, up_full, down_full = (
        lax.all_gather(gains, FSDP, axis=1, tiled=True),
        lax.all_gather(shifts, FSDP, axis=1, tiled=True),
        lax.all_gather(head_bias, FSDP, axis=1, tiled=True),
        lax.all_gather(qkv_weight, FSDP, axis=1, tiled=True),
        lax.all_gather(proj_weight, FSDP, axis=1, tiled=True),
        lax.all_gather(up_weight, FSDP, axis=0, tiled=True),
        lax.all_gather(down_weight, FSDP, axis=1, tiled=True),
    )
    gain_vals = gain_full.astype(jnp.float32)
    shift_vals = shift_full.astype(jnp.float32)
    bias_vals = bias_full[0].astype(jnp.float32)
    tp_width = qkv_full.shape[2]
    local_rows = rows_in.shape[1]
    seq_length = seg_row.shape[1]
    head_local = tp_width // HD
    rows = rows_in[0].astype(jnp.float32)
    row_start = lax.axis_index(CTX) * local_rows
    seg_all = seg_row[0]
    seg_query = lax.dynamic_slice_in_dim(seg_all, row_start, local_rows)
    query_pos = row_start + jnp.arange(local_rows, dtype=jnp.int32)
    key_pos = jnp.arange(seq_length, dtype=jnp.int32)
    allowed = seg_query[:, None] == seg_all[None, :]
    if causal:
        allowed = jnp.logical_and(allowed, key_pos[None, :] <= query_pos[:, None])

    def to_heads(matrix):
        return matrix.reshape(matrix.shape[0], head_local, HD).transpose(1, 0, 2)

    def from_heads(stacked):
        return stacked.transpose(1, 0, 2).reshape(stacked.shape[1], head_local * HD)

    normed_one, inv_one = layer_stats(rows)
    first_in = (normed_one * gain_vals[0] + shift_vals[0]).astype(jnp.bfloat16)
    queries = (
        jnp.dot(first_in, qkv_full[0], preferred_element_type=jnp.float32) + bias_vals[:tp_width]
    ).astype(jnp.bfloat16)
    key_rows = jnp.dot(first_in, qkv_full[1], preferred_element_type=jnp.float32).astype(
        jnp.bfloat16
    )
    values = (
        jnp.dot(first_in, qkv_full[2], preferred_element_type=jnp.float32)
        + bias_vals[tp_width : 2 * tp_width]
    ).astype(jnp.bfloat16)
    key_all, value_all = (
        lax.all_gather(key_rows, CTX, axis=0, tiled=True),
        lax.all_gather(values, CTX, axis=0, tiled=True),
    )
    query_heads = to_heads(queries)
    key_heads = to_heads(key_all)
    value_heads = to_heads(value_all)

    def attend(head_items):
        query_h, key_h, value_h = head_items
        scores = dot(query_h, key_h, ((1,), (1,))) * 0.125
        scores = jnp.where(allowed, scores, -1e30)
        row_top = jnp.max(scores, axis=-1, keepdims=True)
        weights = jnp.exp(scores - row_top)
        row_total = jnp.sum(weights, axis=-1, keepdims=True)
        weights_low = (weights / row_total).astype(jnp.bfloat16)
        mixed_h = dot(weights_low, value_h, ((1,), (0,)))
        return (mixed_h.astype(jnp.bfloat16), row_top[:, 0] + jnp.log(row_total[:, 0]))

    mixed_heads, log_totals = lax.map(attend, (query_heads, key_heads, value_heads))
    mixed = from_heads(mixed_heads)
    middle = (
        rows
        + tensor_psum(jnp.dot(mixed, proj_full, preferred_element_type=jnp.float32))
        + shift_vals[1]
    )
    normed_two, inv_two = layer_stats(middle)
    second_in = (normed_two * gain_vals[1] + shift_vals[2]).astype(jnp.bfloat16)
    hidden = (
        jnp.dot(second_in, up_full, preferred_element_type=jnp.float32) + bias_vals[2 * tp_width :]
    )
    sigma = jax.nn.sigmoid(1.702 * hidden)
    activated = (hidden * sigma).astype(jnp.bfloat16)
    output = (
        middle
        + tensor_psum(jnp.dot(activated, down_full, preferred_element_type=jnp.float32))
        + shift_vals[3]
    )
    grad_out = cotangent[0].astype(jnp.float32)
    grad_down_bias = jnp.sum(grad_out, axis=0)
    grad_branch = grad_out.astype(jnp.bfloat16)
    grad_down = dot(activated, grad_branch, ((0,), (0,)))
    grad_act = dot(grad_branch, down_full, ((1,), (1,)))
    grad_hidden = (grad_act * (sigma + 1.702 * hidden * sigma * (1.0 - sigma))).astype(jnp.bfloat16)
    grad_up_bias = jnp.sum(grad_hidden.astype(jnp.float32), axis=0)
    grad_up = dot(second_in, grad_hidden, ((0,), (0,)))
    grad_second = tensor_psum(
        dot(grad_hidden, up_full, ((1,), (1,)))
    )
    grad_gain_two = jnp.sum(grad_second * normed_two, axis=0)
    grad_shift_two = jnp.sum(grad_second, axis=0)
    grad_middle = grad_out + norm_back(grad_second, normed_two, inv_two, gain_vals[1])
    grad_proj_bias = jnp.sum(grad_middle, axis=0)
    grad_attn = grad_middle.astype(jnp.bfloat16)
    grad_proj = dot(mixed, grad_attn, ((0,), (0,)))
    grad_mixed = dot(grad_attn, proj_full, ((1,), (1,))).astype(jnp.bfloat16)

    def attend_back(head_items):
        query_h, key_h, value_h, grad_h, log_total = head_items
        scores = dot(query_h, key_h, ((1,), (1,))) * 0.125
        weights = jnp.where(allowed, jnp.exp(scores - log_total[:, None]), 0.0)
        grad_weights = dot(grad_h, value_h, ((1,), (1,)))
        row_delta = jnp.sum(weights * grad_weights, axis=-1, keepdims=True)
        grad_scores = (weights * (grad_weights - row_delta)).astype(jnp.bfloat16)
        grad_query_h = (
            dot(grad_scores, key_h, ((1,), (0,))) * 0.125
        )
        grad_key_h = (
            dot(grad_scores, query_h, ((0,), (0,)))
            * 0.125
        )
        grad_value_h = dot(weights.astype(jnp.bfloat16), grad_h, ((0,), (0,)))
        return (grad_query_h, grad_key_h, grad_value_h)

    query_parts, key_parts, value_parts = lax.map(
        attend_back, (query_heads, key_heads, value_heads, to_heads(grad_mixed), log_totals)
    )
    key_sum, value_sum = (
        lax.psum_scatter(from_heads(key_parts), CTX, scatter_dimension=0, tiled=True),
        lax.psum_scatter(from_heads(value_parts), CTX, scatter_dimension=0, tiled=True),
    )
    grad_query = from_heads(query_parts).astype(jnp.bfloat16)
    grad_key = key_sum.astype(jnp.bfloat16)
    grad_value = value_sum.astype(jnp.bfloat16)
    grad_qkv = jnp.stack(
        [
            dot(first_in, grad_query, ((0,), (0,))),
            dot(first_in, grad_key, ((0,), (0,))),
            dot(first_in, grad_value, ((0,), (0,))),
        ]
    )
    grad_head = jnp.concatenate(
        [
            jnp.sum(grad_query.astype(jnp.float32), axis=0),
            jnp.sum(grad_value.astype(jnp.float32), axis=0),
            grad_up_bias,
        ]
    )[None, :]
    grad_first_part = dot(grad_query, qkv_full[0], ((1,), (1,)))
    grad_first_part = grad_first_part + dot(grad_key, qkv_full[1], ((1,), (1,)))
    grad_first_part = grad_first_part + dot(grad_value, qkv_full[2], ((1,), (1,)))
    grad_first = tensor_psum(grad_first_part)
    grad_gain_one = jnp.sum(grad_first * normed_one, axis=0)
    grad_shift_one = jnp.sum(grad_first, axis=0)
    grad_rows = grad_middle + norm_back(grad_first, normed_one, inv_one, gain_vals[0])
    grad_gains = jnp.stack([grad_gain_one, grad_gain_two])
    grad_shifts = jnp.stack([grad_shift_one, grad_proj_bias, grad_shift_two, grad_down_bias])
    share_gains, share_shifts, share_head, share_qkv, share_proj, share_up, share_down = (
        lax.psum_scatter(grad_gains, FSDP, scatter_dimension=1, tiled=True),
        lax.psum_scatter(grad_shifts, FSDP, scatter_dimension=1, tiled=True),
        lax.psum_scatter(grad_head, FSDP, scatter_dimension=1, tiled=True),
        lax.psum_scatter(grad_qkv, FSDP, scatter_dimension=1, tiled=True),
        lax.psum_scatter(grad_proj, FSDP, scatter_dimension=1, tiled=True),
        lax.psum_scatter(grad_up, FSDP, scatter_dimension=0, tiled=True),
        lax.psum_scatter(grad_down, FSDP, scatter_dimension=1, tiled=True),
    )
    owned = lax.psum(
        (share_gains, share_shifts, share_head, share_qkv, share_proj, share_up, share_down), CTX
    )
    return (output.astype(jnp.bfloat16)[None], grad_rows[None]) + tuple(owned)


def on_any_mesh(
    image_input,
    image_segments,
    image_cotangent,
    image_gains,
    image_shifts,
    image_head_bias,
    image_qkv_weight,
    image_proj_weight,
    image_up_weight,
    image_down_weight,
    text_input,
    text_segments,
    text_cotangent,
    text_gains,
    text_shifts,
    text_head_bias,
    text_qkv_weight,
    text_proj_weight,
    text_up_weight,
    text_down_weight,
):
    image_results = any_mesh_block(
        image_input,
        image_segments,
        image_cotangent,
        image_gains,
        image_shifts,
        image_head_bias,
        image_qkv_weight,
        image_proj_weight,
        image_up_weight,
        image_down_weight,
        False,
    )
    text_results = any_mesh_block(
        text_input,
        text_segments,
        text_cotangent,
        text_gains,
        text_shifts,
        text_head_bias,
        text_qkv_weight,
        text_proj_weight,
        text_up_weight,
        text_down_weight,
        True,
    )
    return image_results + text_results


def stream_specs():
    return (
        P(FSDP, CTX, None),
        P(FSDP, None),
        P(FSDP, CTX, None),
        P(None, FSDP),
        P(None, FSDP),
        P(TP, FSDP),
        P(None, FSDP, TP),
        P(TP, FSDP),
        P(FSDP, TP),
        P(TP, FSDP),
    )


def solution(mesh):
    one = stream_specs()
    grads = (one[0], one[0]) + one[3:]
    body = on_device
    if (mesh.shape[FSDP], mesh.shape[CTX], mesh.shape[TP]) != (4, 4, 2):
        body = on_any_mesh
    return jax.shard_map(
        body, mesh=mesh, in_specs=one + one, out_specs=grads + grads, check_vma=False
    )
```

time: 1450 us -> 479 us (0.33)
  waiting for transfers between devices: 962 us -> 15.3 us
  Pallas kernels: 0 us -> 429 us
  matrix products: 238 us -> 0 us
  blocking collectives: 105 us -> 0 us
  local copies, waits for them, and re-layouts: 70.3 us -> 20.3 us
  other arithmetic: 41.6 us -> 7.95 us
  between operations: 16.9 us -> 0.92 us
    reduce_scatter x12 -> x0, waiting for transfers between devices: 438 us -> none  [the longest x2 98.6 us: run_block(): lax.psum_scatter(grad_down, 'fsdp', scatter_dimension=1, tiled=True)]
    pallas_call x0 -> x8, Pallas kernels: none -> 429 us  [the longest x1 188 us: last(): pl.pallas_call(last_kernel, out_shape=out_shape, in_specs=[hbm, hbm, hbm,...]
    dot_general x106 -> x0, matrix products: 238 us -> none  [the longest x10 32.8 us: attend(): jnp.einsum('qk,kd->qd', weights_low, value_h, preferred_element_type=jnp....]
    psum x4 -> x0, waiting for transfers between devices: 208 us -> none  [the longest x1 168 us: run_block(): lax.psum((share_gains, share_shifts, share_head, share_qkv, share_proj, s...]
    unnamed x37 -> x0, waiting for transfers between devices: 164 us -> none
    all_gather x9 -> x0, waiting for transfers between devices: 152 us -> none  [the longest x2 60.4 us: run_block(): lax.all_gather(up_weight, 'fsdp', axis=0, tiled=True)]
    all_gather x8 -> x0, blocking collectives: 74.2 us -> none  [the longest x2 18.3 us: run_block(): lax.all_gather(proj_weight, 'fsdp', axis=1, tiled=True)]
    unnamed x203 -> x28, local copies, waits for them, and re-layouts: 43.6 us -> 7.07 us
  transfers between devices with their start and end apart: 31 -> 4, of which waited for: 26 -> 4; matrix products, arithmetic and copies ran while one was open for 16% -> 0% of each run, Pallas kernels for 0% -> 0%
where the time goes in v2:
time: 479 us; the launch traced here: 478 us
  Pallas kernels  429 us (90%)
  local copies, waits for them, and re-layouts  20.3 us (4%)
  waiting for transfers between devices  15.3 us (3%)
  other arithmetic  7.95 us (2%)
    pallas_call x1, Pallas kernels, last(): pl.pallas_call(last_kernel, out_shape=out_shape, in_specs=[hbm, hbm, hbm,...  188 us
    pallas_call x1, Pallas kernels, front(): pl.pallas_call(front_kernel, out_shape=out_shape, in_specs=[vmem] * 12, o...  98.1 us
    pallas_call x1, Pallas kernels, middle(): pl.pallas_call(middle_kernel, out_shape=out_shape, in_specs=([vmem] * 4 +...  58.4 us
    pallas_call x2, Pallas kernels, attend_back(): pl.pallas_call(functools.partial(attend_back_kernel, causal), grid_spec=p...  42.2 us
    pallas_call x2, Pallas kernels, attend(): pl.pallas_call(functools.partial(attend_kernel, causal), grid_spec=pltpu....  38.3 us
    ppermute x4, waiting for transfers between devices, reduce_small(): lax.ppermute(vector, axis, [(i, i ^ step) for i in range(4)])  15.3 us
  transfers between devices with their start and end apart: 4, of which 4 were waited for; matrix products, arithmetic and copies ran while one was open for 0% of the time, Pallas kernels for 0%

profile of v2, /device:TPU:0, one launch (start us, length us, event | category | flops | bytes accessed | tf_op | source)
XLA Modules:
  0.0 477.5 jit_solution(254383970941883622)
XLA Ops:
  0.7 0.7 convert_element_type.51
  1.4 0.7 convert_element_type.53
  2.1 0.7 convert_element_type.52
  2.8 0.7 constant_dynamic-update-slice_fusion.2
  3.5 0.5 broadcast.345
  4.0 1.4 reduce.9
  5.7 1.4 reduce.8
  7.3 0.2 dynamic_update_slice.23
  7.5 2.0 copy.52.segcol_ref
  9.5 2.0 copy.55.segcol_ref
  11.6 0.2 convert_reduce_fusion.1
  11.8 0.2 convert_reduce_fusion.3
  12.2 0.2 dynamic_update_slice.21
  12.4 0.2 dynamic_update_slice.22
  12.6 0.6 select_maximum_fusion.2.refs_1_
  13.2 0.6 select_maximum_fusion.refs_7_
  13.9 0.6 pad_add_fusion
  14.5 98.1 %front.1 = (bf16[3,512,256]{2,1,0:T(8,128)(2,1)}, f32[16,512]{1,0:T(8,128)}, bf16[512,512]{1,0:T(8,128)(2,1)}, bf16[4,768,128]{2,1,0:T(8,128)(2,1)}, bf16[512,25...) custom-call(bf16[512,512]{1,0:T(8,128)(2,1)} %bitcast.59, ...), custom_call_target="tpu_custom_call" | custom-call | tf_op jit(solution)/shard_map/front/pallas_call | solution.py:533
  112.6 16.0 %attend_causal.1 = (bf16[4,256,128]{2,1,0:T(8,128)(2,1)}, f32[8,16,256]{2,1,0:T(8,128)}) custom-call(s32[3,8]{1,0:T(4,128)} %get-tuple-element.127.bounds, bf16[4,768,128]{2,1,0:T(8,128)(2,1)} %get-tuple-element.68.m_ref, s32[2048,1]{1,0:T(8,128)} %copy.52.segcol_ref, s32[1,2048]{1,0:T(1,128)} %segrow_ref.6), custom_call_target="tpu_custom_call" | custom-call | flops 2147483648 | bytes 1572864 | tf_op jit(solution)/shard_map/attend_causal/pallas_call | solution.py:114
  128.6 22.2 %attend_full.1 = (bf16[4,512,128]{2,1,0:T(8,128)(2,1)}, f32[8,16,256]{2,1,0:T(8,128)}) custom-call(s32[3,8]{1,0:T(4,128)} %get-tuple-element.126.bounds, bf16[4,3,512,128]{3,2,1,0:T(8,128)(2,1)} %get-tuple-element.74.m_ref, s32[2048,1]{1,0:T(8,128)} %copy.55.segcol_ref, s32[1,2048]{1,0:T(1,128)} %segrow_ref.7), custom_call_target="tpu_custom_call" | custom-call | flops 4294967296 | bytes 1572864 | tf_op jit(solution)/shard_map/attend_full/pallas_call | solution.py:114
  150.8 58.4 %middle.1 = (bf16[512,512]{1,0:T(8,128)(2,1)}, f32[512,512]{1,0:T(8,128)}, bf16[4,256,128]{2,1,0:T(8,128)(2,1)}, bf16[512,2304]{1,0:T(8,128)(2,1)}, f32[16,512]{...) custom-call(bf16[4,256,128]{2,1,0:T(8,128)(2,1)} %get-tuple-element., ...), custom_call_target="tpu_custom_call" | custom-call | tf_op jit(solution)/shard_map/middle/pallas_call | solution.py:762
  209.2 23.7 %attend_back_full.1.refs_8_ = bf16[4,3,512,128]{3,2,1,0:T(8,128)(2,1)} custom-call(s32[3,8]{1,0:T(4,128)} %get-tuple-element.126.bounds, bf16[4,3,512,128]{3,2,1,0:T(8,128)(2,1)} %get-tuple-element.74.m_ref, bf16[4,512,128]{2,1,0:T(8,128)(2,1)} %get-tuple-element.88.do_ref, bf16[4,512,128]{2,1,0:T(8,128)(2,1)} %get-tuple-element.75.refs_7_.o_ref, ...), custom_call_target="tpu_custom_call" | custom-call | flops 10737418240 | bytes 3145728 | tf_op jit(solution)/shard_map/attend_back_full/pallas_call | solution.py:253
  232.9 18.5 %attend_back_causal.1.refs_0_ = bf16[4,768,128]{2,1,0:T(8,128)(2,1)} custom-call(s32[3,8]{1,0:T(4,128)} %get-tuple-element.127.bounds, bf16[4,768,128]{2,1,0:T(8,128)(2,1)} %get-tuple-element.68.m_ref, bf16[4,256,128]{2,1,0:T(8,128)(2,1)} %get-tuple-element.81.do_ref, bf16[4,256,128]{2,1,0:T(8,128)(2,1)} %get-tuple-element.69.refs_0_.o_ref, ...), custom_call_target="tpu_custom_call" | custom-call | flops 5368709120 | bytes 3145728 | tf_op jit(solution)/shard_map/attend_back_causal/pallas_call | solution.py:253
  251.4 188.3 %last.1 = (f32[512,512]{1,0:T(8,128)}, f32[16,512]{1,0:T(8,128)}, bf16[128,2304]{1,0:T(8,128)(2,1)}, bf16[128,768]{1,0:T(8,128)(2,1)}, f32[512,768]{1,0:T(8,128)...) custom-call(bf16[4,768,128]{2,1,0:T(8,128)(2,1)} %attend_back_causal.1.refs_0_, ...), custom_call_target="tpu_custom_call" | custom-call | tf_op jit(solution)/shard_map/last/pallas_call | solution.py:1086
  439.7 0.8 constant_dynamic-update-slice_fusion.1
  440.5 0.8 constant_dynamic-update-slice_fusion
  441.3 4.4 collective-permute-done
  445.8 4.4 collective-permute-done.1
  450.3 1.0 collective-permute-start.2
  451.3 3.5 collective-permute-done.2
  454.8 2.4 collective-permute-start.3
  457.2 3.0 collective-permute-done.3
  460.2 0.6 slice.28.refs_0_
  460.8 0.6 slice.29.refs_3_
  461.4 4.3 finish.1
  465.7 1.3 constant_dynamic-slice_fusion.5
  467.0 1.4 constant_dynamic-slice_fusion.4
  468.4 1.2 constant_dynamic-slice_fusion.2
  469.6 1.2 constant_dynamic-slice_fusion.1
  470.8 0.7 copy.63
  471.5 0.6 constant_dynamic-slice_fusion
  472.1 0.7 copy.62
  472.8 0.7 constant_dynamic-slice_fusion.3
  473.5 0.9 copy.75
  474.4 1.1 copy.76
  475.5 0.2 copy-done.3
  475.7 0.8 copy.77
  476.5 1.0 copy.78
  (44 shorter events, 0.8 us)
Async XLA Ops:
  0.7 10.9 %copy-start.4 = (s32[1,2048]{1,0:T(1,128)S(1)}, s32[1,2048]{1,0:T(1,128)}, u32[]{:S(2)}) copy-start(s32[1,2048]{1,0:T(1,128)} %segrow_ref.7) | copy-start | bytes 24580
  0.7 11.2 %copy-start.5 = (s32[1,2048]{1,0:T(1,128)S(1)}, s32[1,2048]{1,0:T(1,128)}, u32[]{:S(2)}) copy-start(s32[1,2048]{1,0:T(1,128)} %segrow_ref.6) | copy-start | bytes 24580
  0.7 11.4 %copy-start.7 = (bf16[2,128]{1,0:T(2,128)(2,1)S(1)}, bf16[2,128]{1,0:T(2,128)(2,1)}, u32[]{:S(2)}) copy-start(bf16[2,128]{1,0:T(2,128)(2,1)} %param.33) | copy-start | bytes 1540
  0.7 11.4 %copy-start.6 = (bf16[4,128]{1,0:T(4,128)(2,1)S(1)}, bf16[4,128]{1,0:T(4,128)(2,1)}, u32[]{:S(2)}) copy-start(bf16[4,128]{1,0:T(4,128)(2,1)} %param.34) | copy-start | bytes 3076
  441.3 4.4 collective-permute-start
  445.7 4.5 collective-permute-start.1
  450.3 4.5 collective-permute-start.2
  454.8 5.4 %collective-permute-start.3 = (f32[16,1280]{1,0:T(8,128)S(1)}, f32[16,1280]{1,0:T(8,128)S(1)}, u32[]{:S(2)}, u32[]{:S(2)}) collective-permute-start(f32[16,1280]{1,0:T(8,128)S(1)} %add.124), channel_id=1, source_target_pairs={{0,4},{2,6},{4,0},{6,2},{1,5},{3,7},{5,1},{7,3},{8,12},{10,14},{12... | collective-permute-start | bytes 245768 | tf_op jit(solution)/shard_map/ppermute | solution.py:27
  457.2 16.3 %copy-start.2 = (bf16[512,768]{1,0:T(8,128)(2,1)S(1)}, bf16[512,768]{1,0:T(8,128)(2,1)}, u32[]{:S(2)}) copy-start(bf16[512,768]{1,0:T(8,128)(2,1)} %get-tuple-element.80) | copy-start | bytes 2359300
  461.4 12.9 %copy-start = (f32[512,768]{1,0:T(8,128)S(1)}, f32[512,768]{1,0:T(8,128)}, u32[]{:S(2)}) copy-start(f32[512,768]{1,0:T(8,128)} %get-tuple-element.95) | copy-start | bytes 4718596
  474.4 1.4 copy-start.3
  474.4 2.2 copy-start.1
